TPU v7x, 256 devices: a whole 4x4x8 slice. The times are simulated.
256 devices in a mesh: dp: 4 (over y), ctx: 64 (over z, x, core).
Axes of the slice: x: 4, y: 4, z: 8, core: 2. Of those that a mesh axis runs over, the one named last changes fastest.
Arguments:
- projected: bfloat16 [4, 8192, 12288], P('dp', 'ctx'), may hold values from -6 to 6
- doc_ids: int32 [4, 8192], P('dp'), may hold values from 0 to 15, never falling along the last dimension, each value on 1 to 1024 neighbouring positions
- short_filter: float32 [3, 12288], replicated, may hold values from -3.5 to 3.5
- long_filter: bfloat16 [256, 128], replicated, may hold values from -0.5 to 0.5
- cotangent: bfloat16 [4, 8192, 4096], P('dp', 'ctx'), may hold values from -6 to 6
Outputs:
- block_out: bfloat16 [4, 8192, 4096], P('dp', 'ctx')
- grad_projected: bfloat16 [4, 8192, 12288], P('dp', 'ctx')
- grad_short: float32 [3, 12288], P(None, 'ctx')
- grad_long: float32 [256, 128], P('ctx')
Inputs may be any that keep to these rules, and one draw needn't show every extreme that they name: `doc_ids`: document numbers never fall along a row, each document spans 1 to 1024 positions, and some document spans exactly 1024.
All inputs are finite; a program needn't handle non-finite values.
Results may differ from a plain program's by a relative error of at most 0.0076.
Values may be sent and summed in bfloat16 or wider, within the bound.
A program may use at most 256 MiB of HBM per device.

v0:
```python
import functools
import math

import jax
import jax.numpy as jnp
from jax import lax
from jax.experimental import pallas as pl
from jax.experimental.pallas import tpu as pltpu
from jax.sharding import PartitionSpec as P

BF = jnp.bfloat16
F32 = jnp.float32
ROWS = 32
LANES = 128


def passed_along(value, axis, steps):
    count = lax.axis_size(axis)
    first, last = (max(0, -steps), min(count, count - steps))
    return lax.ppermute(value, axis, [(s, s + steps) for s in range(first, last)])


def same(cols, other):
    return cols[:, 0:1] == cols[:, other : other + 1]


def mix_kernel(cols_ref, q_ref, k_ref, v_ref, bq_ref, bk_ref, bv_ref, wq_ref, wk_ref, wv_ref, cot_ref,
               q_out, k_out, v_out, prod_ref, gm_ref, ext):
    cols = cols_ref[...]
    tok = q_ref.shape[0]
    one, two = same(cols, 1), same(cols, 2)

    def mixed(x_ref, b_ref, w_ref, out):
        x = x_ref[...].astype(F32)
        ext[6:8, :] = b_ref[...].astype(F32)
        ext[8 : 8 + tok, :] = x
        total = w_ref[0:1, :] * x
        total = total + jnp.where(one, w_ref[1:2, :] * ext[7 : 7 + tok, :], 0.0)
        total = total + jnp.where(two, w_ref[2:3, :] * ext[6 : 6 + tok, :], 0.0)
        rounded = total.astype(BF)
        out[...] = rounded
        return rounded.astype(F32)

    gm_ref[...] = (cot_ref[...].astype(F32) * mixed(q_ref, bq_ref, wq_ref, q_out)).astype(BF)
    key = mixed(k_ref, bk_ref, wk_ref, k_out)
    prod_ref[...] = (key * mixed(v_ref, bv_ref, wv_ref, v_out)).astype(BF)


def banded(filters, rows):
    parts = []
    for g in range(filters.shape[0]):
        wide = jnp.broadcast_to(filters[g : g + 1, :], (rows, filters.shape[1]))
        parts.append(pltpu.roll(wide, 0, 1, stride=1, stride_axis=0))
    return jnp.concatenate(parts, axis=0).astype(BF)


def window(first, second, start, size):
    tok = first.shape[0]
    if start + size <= tok:
        return first[start : start + size]
    return jnp.concatenate([first[start:], second[: start + size - tok]], axis=0)


def long_kernel(groups, cols_ref, dwin_ref, filt_ref, q_ref, k_ref, v_ref, cot_ref, prod_ref, gm_ref,
                before_ref, after_ref, out_ref, mg_ref, gl_ref):
    rows = ROWS
    tok, width = q_ref.shape
    steps = tok // rows
    reach = rows + tok
    lane_group = lax.broadcasted_iota(jnp.int32, (rows, LANES), 1) // (LANES // groups)
    docs = cols_ref[:, 0:1]
    masks = [docs[(a % steps) * rows : (a % steps + 1) * rows] == dwin_ref[a : a + 1, :] for a in range(2 * steps)]
    masks = [jnp.where(m, 1.0, 0.0) for m in masks]

    def block(i, carry):
        at = pl.ds(pl.multiple_of(i * LANES, LANES), LANES)
        filt = filt_ref[pl.ds(pl.multiple_of(i * groups, groups), groups), :]
        prod, gm = prod_ref[:, at], gm_ref[:, at]
        before, after = before_ref[:, at], after_ref[:, at]

        def pick(value):
            total = value[:rows]
            for g in range(1, groups):
                total = jnp.where(lane_group == g, value[g * rows : (g + 1) * rows], total)
            return total

        ahead = banded(filt[:, : 2 * tok], rows)
        back = banded(filt[:, 2 * tok :], rows)
        diag = jnp.zeros((groups * rows, reach), F32)
        for a in range(steps):
            here = slice(a * rows, (a + 1) * rows)
            keep = jnp.concatenate([masks[a].astype(BF)] * groups, axis=0)
            mix = jnp.dot((ahead * keep)[:, :reach], window(before, prod, a * rows, reach), preferred_element_type=F32)
            mix = pick(mix).astype(BF).astype(F32)
            out_ref[here, at] = (q_ref[here, at].astype(F32) * mix).astype(BF)
            mg_ref[0, here, at] = (cot_ref[here, at].astype(F32) * mix).astype(BF)
            keep32 = jnp.concatenate([masks[steps + a]] * groups, axis=0)
            span = window(gm, after, a * rows, reach)
            gp = jnp.dot((back * keep32.astype(BF))[:, :reach], span, preferred_element_type=F32)
            gp = pick(gp).astype(BF).astype(F32)
            mg_ref[1, here, at] = (gp * v_ref[here, at].astype(F32)).astype(BF)
            mg_ref[2, here, at] = (gp * k_ref[here, at].astype(F32)).astype(BF)
            mine = prod[here]
            spread = jnp.concatenate([jnp.where(lane_group == g, mine, jnp.zeros_like(mine)) for g in range(groups)], axis=0)
            pairs = lax.dot_general(spread, span, (((1,), (1,)), ((), ())), preferred_element_type=F32)
            diag = diag + pairs * keep32[:, :reach]
        diag = jnp.concatenate([diag, jnp.zeros((groups * rows, 2 * tok - reach), F32)], axis=1)
        fold = diag.reshape(groups, rows, 2 * tok)
        half = rows // 2
        while half >= 8:
            fold = fold[:, :half] + pltpu.roll(fold[:, half:], 2 * tok - half, 2)
            half //= 2
        while half >= 1:
            fold = fold + pltpu.roll(pltpu.roll(fold, 8 - half, 1), 2 * tok - half, 2)
            half //= 2
        gl_ref[pl.ds(pl.multiple_of(i * groups, groups), groups), :] = fold[:, 0, :tok]
        return carry

    lax.fori_loop(0, width // LANES, block, 0)


def close_kernel(cols_ref, mg_ref, next_ref, x_ref, b_ref, w_ref, out_ref, gs_ref, ext, grad):
    cols = cols_ref[...]
    tok = x_ref.shape[0]
    g = mg_ref[0].astype(F32)
    grad[0:tok, :] = g
    grad[tok : tok + 2, :] = next_ref[0].astype(F32)
    x = x_ref[...].astype(F32)
    ext[6:8, :] = b_ref[...].astype(F32)
    ext[8 : 8 + tok, :] = x
    total = w_ref[0:1, :] * g
    total = total + jnp.where(same(cols, 3), w_ref[1:2, :] * grad[1 : 1 + tok, :], 0.0)
    total = total + jnp.where(same(cols, 4), w_ref[2:3, :] * grad[2 : 2 + tok, :], 0.0)
    out_ref[...] = total.astype(BF)
    gs_ref[0:1, :] = jnp.sum(g * x, axis=0, keepdims=True)
    gs_ref[1:2, :] = jnp.sum(jnp.where(same(cols, 1), g * ext[7 : 7 + tok, :], 0.0), axis=0, keepdims=True)
    gs_ref[2:3, :] = jnp.sum(jnp.where(same(cols, 2), g * ext[6 : 6 + tok, :], 0.0), axis=0, keepdims=True)


def tables(doc_row, first, tok):
    span = 4 * tok
    padded = jnp.concatenate([jnp.full((tok,), -1, jnp.int32), doc_row, jnp.full((2 * tok,), -2, jnp.int32)])
    near = lax.dynamic_slice_in_dim(padded, first, span, 0)
    cols = jnp.stack([near[tok + d : 2 * tok + d] for d in (0, -1, -2, 1, 2, 0, 0, 0)], axis=1)
    dwin = jnp.stack([near[a * ROWS : a * ROWS + 2 * tok] for a in range(2 * tok // ROWS)], axis=0)
    return cols, dwin


def wide_filters(long_filter):
    taps = long_filter.shape[1]
    f = long_filter.astype(F32)
    return jnp.concatenate(
        [jnp.pad(f[:, ::-1], ((0, 0), (1, taps - 1))), jnp.pad(f, ((0, 0), (0, taps)))], axis=1
    )


def mix_call(cols, x, border, w, cot, chunk):
    tok, width = cot.shape
    n = width // chunk
    third = [lambda i, p=p: (0, p * n + i) for p in range(3)]
    flat = lambda i: (0, i)
    shape = jax.ShapeDtypeStruct((tok, width), BF)
    return pl.pallas_call(
        mix_kernel,
        grid=(n,),
        out_shape=[shape] * 5,
        in_specs=[pl.BlockSpec((tok, 8), lambda i: (0, 0))]
        + [pl.BlockSpec((tok, chunk), m) for m in third]
        + [pl.BlockSpec((2, chunk), m) for m in third]
        + [pl.BlockSpec((3, chunk), m) for m in third]
        + [pl.BlockSpec((tok, chunk), flat)],
        out_specs=[pl.BlockSpec((tok, chunk), flat)] * 5,
        scratch_shapes=[pltpu.VMEM((8 + tok, chunk), F32)],
        compiler_params=pltpu.CompilerParams(vmem_limit_bytes=48 << 20),
        name="mix",
    )(cols, x, x, x, border, border, border, w, w, w, cot)


def long_call(cols, dwin, filt, q, k, v, cot, prod, gm, before, after, groups_total, chunk):
    tok, width = cot.shape
    per = width // groups_total
    n = width // chunk
    flat = pl.BlockSpec((tok, chunk), lambda i: (0, i))
    return pl.pallas_call(
        functools.partial(long_kernel, LANES // per),
        grid=(n,),
        out_shape=[
            jax.ShapeDtypeStruct((tok, width), BF),
            jax.ShapeDtypeStruct((3, tok, width), BF),
            jax.ShapeDtypeStruct((groups_total, tok), F32),
        ],
        in_specs=[
            pl.BlockSpec((tok, 8), lambda i: (0, 0)),
            pl.BlockSpec(dwin.shape, lambda i: (0, 0)),
            pl.BlockSpec((chunk // per, 4 * tok), lambda i: (i, 0)),
        ]
        + [flat] * 8,
        out_specs=[
            flat,
            pl.BlockSpec((3, tok, chunk), lambda i: (0, 0, i)),
            pl.BlockSpec((chunk // per, tok), lambda i: (i, 0)),
        ],
        compiler_params=pltpu.CompilerParams(vmem_limit_bytes=48 << 20),
        name="long",
    )(cols, dwin, filt, q, k, v, cot, prod, gm, before, after)


def close_call(cols, mg, ahead, x, border, w, chunk):
    tok, width = x.shape
    n = mg.shape[2] // chunk
    third = lambda p, i: (0, p * n + i)
    return pl.pallas_call(
        close_kernel,
        grid=(3, n),
        out_shape=[jax.ShapeDtypeStruct((tok, width), BF), jax.ShapeDtypeStruct((3, width), F32)],
        in_specs=[
            pl.BlockSpec((tok, 8), lambda p, i: (0, 0)),
            pl.BlockSpec((1, tok, chunk), lambda p, i: (p, 0, i)),
            pl.BlockSpec((1, 2, chunk), lambda p, i: (p, 0, i)),
            pl.BlockSpec((tok, chunk), third),
            pl.BlockSpec((2, chunk), third),
            pl.BlockSpec((3, chunk), third),
        ],
        out_specs=[pl.BlockSpec((tok, chunk), third), pl.BlockSpec((3, chunk), third)],
        scratch_shapes=[pltpu.VMEM((8 + tok, chunk), F32), pltpu.VMEM((8 + tok, chunk), F32)],
        compiler_params=pltpu.CompilerParams(vmem_limit_bytes=48 << 20),
        name="close",
    )(cols, mg, ahead, x, border, w)


def local(projected, doc_ids, short_filter, long_filter, cotangent):
    x, cot = projected[0], cotangent[0]
    tok, width = cot.shape
    groups, taps = long_filter.shape
    parts = lax.axis_size("ctx")
    cols, dwin = tables(doc_ids[0], lax.axis_index("ctx") * tok, tok)
    border = passed_along(x[tok - 2 :], "ctx", 1)
    q, k, v, prod, gm = mix_call(cols, x, border, short_filter, cot, 512)
    before = passed_along(prod, "ctx", 1)
    after = passed_along(gm, "ctx", -1)
    out, mg, gl = long_call(
        cols, dwin, wide_filters(long_filter), q, k, v, cot, prod, gm, before, after, groups, 512
    )
    ahead = passed_along(mg[:, :2], "ctx", -1)
    gx, gs = close_call(cols, mg, ahead, x, border, short_filter, 512)
    own_s, own_l = gs.shape[1] // parts, groups // parts
    packed = jnp.concatenate(
        [gs.reshape(3, parts, own_s).transpose(1, 0, 2).reshape(parts, -1), gl.reshape(parts, -1)], axis=1
    )
    total = lax.psum(lax.psum_scatter(packed, "ctx", scatter_dimension=0, tiled=True), "dp")[0]
    norm = lax.axis_size("dp") * doc_ids.shape[1]
    grad_short = total[: 3 * own_s].reshape(3, own_s) / math.sqrt(norm)
    grad_long = total[3 * own_s :].reshape(own_l, taps) / math.sqrt(norm * (width // groups))
    return out[None], gx[None], grad_short, grad_long


def solution(mesh):
    return jax.shard_map(
        local,
        mesh=mesh,
        in_specs=(P("dp", "ctx", None), P("dp", None), P(), P(), P("dp", "ctx", None)),
        out_specs=(P("dp", "ctx", None), P("dp", "ctx", None), P(None, "ctx"), P("ctx", None)),
        check_vma=False,
    )
```

profile of v0, /device:TPU:1, one launch (start us, length us, event | category | flops | bytes accessed | tf_op | source)
XLA Modules:
  0.0 312.7 jit_solution(15056594036541007547)
XLA Ops:
  7.2 0.0 all-reduce.5.cloned.1.call-start
  7.2 1.0 slice_bitcast_fusion
  8.2 4.5 %collective-permute-start = (bf16[2,12288]{1,0:T(2,128)(2,1)S(1)}, bf16[2,12288]{1,0:T(2,128)(2,1)S(1)}, u32[]{:S(2)}, u32[]{:S(2)}) collective-permute-start(bf16[2,12288]{1,0:T(2,128)(2,1)S(1)} %slice_bitcast_fusion), channel_id=1, source_target_pairs={{0,1},{1,2},{2,3},{3,4},{4,5},{5,6},{6,7},{7,8},{8,9},{9,10},{10,1... | collective-permute-start | bytes 147464 | tf_op jit(solution)/shard_map/ppermute | solution.py:20
  12.7 0.8 fusion.2
  13.5 0.1 slice_bitcast_fusion.1
  13.6 0.1 copy.27.cols_ref
  13.8 0.1 collective-permute-done.bq_ref.bk_ref.bv_ref.b_ref
  13.9 0.0 copy-start.2
  13.9 0.9 copy-done.2
  14.8 0.0 copy-start.7
  14.8 0.0 copy-start
  14.8 8.5 %mix.1 = (bf16[128,4096]{1,0:T(8,128)(2,1)S(1)}, bf16[128,4096]{1,0:T(8,128)(2,1)S(1)}, bf16[128,4096]{1,0:T(8,128)(2,1)S(1)}, bf16[128,4096]{1,0:T(8,128)(2,1)}, bf16[128,4096]{1,0:T(8,128)(2,1)}) custom-call(s32[128,8]{1,0:T(8,128)S(1)} %copy.27.cols_ref, bf16[128,12288]{1,0:T(8,128)(2,1)} %bitcast.32, bf16[128,12288]{1,0:T(8,128)(2,1)} %bitcast.33, ...), custom_call_target="tpu_custom_call" | custom-call | tf_op jit(solution)/shard_map/mix/pallas_call | solution.py:163
  23.3 0.0 copy-start.4
  23.3 1.0 copy-done.4
  24.3 4.2 %collective-permute-start.1 = (bf16[128,4096]{1,0:T(8,128)(2,1)}, bf16[128,4096]{1,0:T(8,128)(2,1)}, u32[]{:S(2)}, u32[]{:S(2)}) collective-permute-start(bf16[128,4096]{1,0:T(8,128)(2,1)} %get-tuple-element.17.prod_ref), channel_id=1, source_target_pairs={{0,1},{1,2},{2,3},{3,4},{4,5},{5,6},{6,7},{7,8},{8,9},{9,10},{10,1... | collective-permute-start | bytes 3145736 | tf_op jit(solution)/shard_map/ppermute | solution.py:20
  28.6 1.9 collective-permute-start.2
  30.5 0.0 copy-done.7
  30.5 0.8 rev.3
  31.3 0.1 fusion.3
  31.4 1.0 select_maximum_fusion.filt_ref
  32.5 8.1 %collective-permute-done.1.before_ref = bf16[128,4096]{1,0:T(8,128)(2,1)} collective-permute-done((bf16[128,4096]{1,0:T(8,128)(2,1)}, bf16[128,4096]{1,0:T(8,128)(2,1)}, u32[]{:S(2)}, u32[]{:S(2)}) %collective-permute-start.1) | collective-permute-done | bytes 1048608 | tf_op jit(solution)/shard_map/ppermute | solution.py:20
  40.6 4.4 %collective-permute-done.2.after_ref = bf16[128,4096]{1,0:T(8,128)(2,1)} collective-permute-done((bf16[128,4096]{1,0:T(8,128)(2,1)}, bf16[128,4096]{1,0:T(8,128)(2,1)}, u32[]{:S(2)}, u32[]{:S(2)}) %collective-permute-start.2) | collective-permute-done | bytes 1048608 | tf_op jit(solution)/shard_map/ppermute | solution.py:20
  45.0 0.0 copy-done
  45.0 0.0 copy-start.5
  45.0 1.2 copy-done.5
  46.2 0.0 copy-start.3
  46.2 34.1 %long.1 = (bf16[128,4096]{1,0:T(8,128)(2,1)}, bf16[3,128,4096]{2,1,0:T(8,128)(2,1)}, f32[256,128]{1,0:T(8,128)S(1)}) custom-call(s32[128,8]{1,0:T(8,128)S(1)} %copy.27.cols_ref, s32[8,256]{1,0:T(8,128)S(1)} %stack.62.dwin_ref, f32[256,512]{1,0:T(8,128)S(1)} %select_maximum_fusion.filt_ref, bf16[128,4096]{1,0:T(8,128)(2,1)S(1)} %get-tuple-element.14.q_ref, ...), custom_call_target="tpu_custom_call" | custom-call | tf_op jit(solution)/shard_map/long/pallas_call | solution.py:184
  80.3 0.0 copy-start.6
  80.3 0.6 copy-done.6
  81.0 1.0 slice.74
  81.9 1.9 collective-permute-start.3
  83.9 0.9 reshape.30
  84.8 2.5 collective-permute-done.3.next_ref
  87.4 0.0 copy-done.3
  87.4 1.9 copy-done.1
  89.3 16.8 %close.1 = (bf16[128,12288]{1,0:T(8,128)(2,1)}, f32[3,12288]{1,0:T(4,128)S(1)}) custom-call(s32[128,8]{1,0:T(8,128)S(1)} %copy.27.cols_ref, bf16[3,128,4096]{2,1,0:T(8,128)(2,1)S(1)} %copy-done.1, bf16[3,2,4096]{2,1,0:T(2,128)(2,1)S(1)} %collective-permute-done.3.next_ref, bf16[128,12288]{1,0:T(8,128)(2,1)} %bitcast.35, ...), custom_call_target="tpu_custom_call" | custom-call | tf_op jit(solution)/shard_map/close/pallas_call | solution.py:212
  106.1 0.1 reshape.28
  106.2 0.1 copy.31
  106.3 0.2 reshape.29
  106.5 0.8 pad_maximum_fusion
  107.3 0.0 all-reduce.5.cloned.1.call-update
  107.4 0.0 copy-done.8
  107.4 0.6 dynamic-slice
  107.9 186.6 %all-reduce.5.cloned.1.call-done = f32[64,1088]{1,0:T(8,128)} async-done(((f32[64,1088]{1,0:T(8,128)}), f32[64,1088]{1,0:T(8,128)}) %all-reduce.5.cloned.1.call-update) | async-done | bytes 278544
  294.5 1.4 constant_dynamic-slice_fusion
  296.0 8.5 %psum.7 = f32[1,1088]{1,0:T(1,128)S(1)} all-reduce(f32[1,1088]{1,0:T(1,128)S(1)} %constant_dynamic-slice_fusion), channel_id=1, replica_groups=mesh['dp'=4,'ctx'=64] {'dp'}, use_global_device_ids=true, to_apply=%region_1.2 | all-reduce | flops 1088 | bytes 8704 | tf_op jit(solution)/shard_map/psum | solution.py:250
  304.5 0.7 slice_multiply_fusion.1
  305.2 0.7 div.18
  (8 shorter events, 0.1 us)
Async XLA Ops:
  7.2 287.4 %all-reduce.5.cloned.1.call-start = ((), (), s32[]{:S(2)}) async-start(), calls=%async_computation | async-start | bytes 589824
  8.2 5.7 %collective-permute-start = (bf16[2,12288]{1,0:T(2,128)(2,1)S(1)}, bf16[2,12288]{1,0:T(2,128)(2,1)S(1)}, u32[]{:S(2)}, u32[]{:S(2)}) collective-permute-start(bf16[2,12288]{1,0:T(2,128)(2,1)S(1)} %slice_bitcast_fusion), channel_id=1, source_target_pairs={{0,1},{1,2},{2,3},{3,4},{4,5},{5,6},{6,7},{7,8},{8,9},{9,10},{10,1... | collective-permute-start | bytes 147464 | tf_op jit(solution)/shard_map/ppermute | solution.py:20
  13.9 0.9 copy-start.2
  14.8 15.7 %copy-start.7 = (bf16[256,128]{1,0:T(8,128)(2,1)S(1)}, bf16[256,128]{1,0:T(8,128)(2,1)}, u32[]{:S(2)}) copy-start(bf16[256,128]{1,0:T(8,128)(2,1)} %param.8) | copy-start | bytes 196612
  14.8 30.2 %copy-start = (bf16[1,128,4096]{2,1,0:T(8,128)(2,1)S(1)}, bf16[1,128,4096]{2,1,0:T(8,128)(2,1)}, u32[]{:S(2)}) copy-start(bf16[1,128,4096]{2,1,0:T(8,128)(2,1)} %param.9) | copy-start | bytes 3145732
  23.3 1.0 copy-start.4
  24.3 16.3 %collective-permute-start.1 = (bf16[128,4096]{1,0:T(8,128)(2,1)}, bf16[128,4096]{1,0:T(8,128)(2,1)}, u32[]{:S(2)}, u32[]{:S(2)}) collective-permute-start(bf16[128,4096]{1,0:T(8,128)(2,1)} %get-tuple-element.17.prod_ref), channel_id=1, source_target_pairs={{0,1},{1,2},{2,3},{3,4},{4,5},{5,6},{6,7},{7,8},{8,9},{9,10},{10,1... | collective-permute-start | bytes 3145736 | tf_op jit(solution)/shard_map/ppermute | solution.py:20
  28.6 16.4 %collective-permute-start.2 = (bf16[128,4096]{1,0:T(8,128)(2,1)}, bf16[128,4096]{1,0:T(8,128)(2,1)}, u32[]{:S(2)}, u32[]{:S(2)}) collective-permute-start(bf16[128,4096]{1,0:T(8,128)(2,1)} %get-tuple-element.18.gm_ref), channel_id=1, source_target_pairs={{1,0},{2,1},{3,2},{4,3},{5,4},{6,5},{7,6},{8,7},{9,8},{10,9},{11,1... | collective-permute-start | bytes 3145736 | tf_op jit(solution)/shard_map/ppermute | solution.py:20
  45.0 1.2 copy-start.5
  46.2 41.1 %copy-start.3 = (f32[3,12288]{1,0:T(4,128)S(1)}, f32[3,12288]{1,0:T(4,128)}, u32[]{:S(2)}) copy-start(f32[3,12288]{1,0:T(4,128)} %w_ref.1) | copy-start | bytes 442372
  80.3 0.6 copy-start.6
  81.9 5.4 %collective-permute-start.3 = (bf16[3,2,4096]{2,1,0:T(2,128)(2,1)S(1)}, bf16[3,2,4096]{2,1,0:T(2,128)(2,1)S(1)}, u32[]{:S(2)}, u32[]{:S(2)}) collective-permute-start(bf16[3,2,4096]{2,1,0:T(2,128)(2,1)S(1)} %slice.74), channel_id=1, source_target_pairs={{1,0},{2,1},{3,2},{4,3},{5,4},{6,5},{7,6},{8,7},{9,8},{10,9},{11,1... | collective-permute-start | bytes 147464 | tf_op jit(solution)/shard_map/ppermute | solution.py:20
  87.4 1.9 copy-start.1
  89.3 18.1 %copy-start.8 = (u32[256]{0:T(256)S(1)}, u32[256]{0:T(256)}, u32[]{:S(2)}) copy-start(u32[256]{0:T(256)} %constant.31) | copy-start | bytes 3076
Sparse Core Ops, SparseCore 0:
  107.5 187.0 all-reduce.4
where the time goes:
time: 315 us; the launch traced here: 313 us
  waiting for transfers between devices  202 us (64%)
  Pallas kernels  59.5 us (19%)
  between operations  14.2 us (5%)
  local copies, waits for them, and re-layouts  12.8 us (4%)
  starting transfers between devices  12.6 us (4%)
  blocking collectives  8.54 us (3%)
  other arithmetic  3.34 us (1%)
    unnamed x2, waiting for transfers between devices  187 us
    pallas_call x1, Pallas kernels, long_call(): pl.pallas_call(functools.partial(long_kernel, LANES // per), grid=(n,), o...  34.1 us
    pallas_call x1, Pallas kernels, close_call(): pl.pallas_call(close_kernel, grid=(3, n), out_shape=[jax.ShapeDtypeStruct...  16.8 us
    ppermute x4, waiting for transfers between devices, passed_along(): lax.ppermute(value, axis, [(s, s + steps) for s in range(first, last)])  15.2 us
    ppermute x4, starting transfers between devices, passed_along(): lax.ppermute(value, axis, [(s, s + steps) for s in range(first, last)])  12.6 us
    psum x1, blocking collectives, local(): lax.psum(lax.psum_scatter(packed, 'ctx', scatter_dimension=0, tiled=True)...  8.54 us
    pallas_call x1, Pallas kernels, mix_call(): pl.pallas_call(mix_kernel, grid=(n,), out_shape=[shape] * 5, in_specs=[pl...  8.54 us
    unnamed x20, local copies, waits for them, and re-layouts  7.68 us
  transfers between devices with their start and end apart: 5, of which 5 were waited for; matrix products, arithmetic and copies ran while one was open for 1% of the time, Pallas kernels for 0%

commit v1 on v0

v1 whole, which is shorter than its diff:
```python
import functools
import math

import jax
import jax.numpy as jnp
from jax import lax
from jax.experimental import pallas as pl
from jax.experimental.pallas import tpu as pltpu
from jax.sharding import PartitionSpec as P

BF = jnp.bfloat16
F32 = jnp.float32
MESH = pl.DeviceIdType.MESH
ROWS = 16
LANES = 128
CORES = 2
ACROSS = 4
VMEM = 56 << 20


def passed_along(value, axis, steps):
    count = lax.axis_size(axis)
    first, last = (max(0, -steps), min(count, count - steps))
    return lax.ppermute(value, axis, [(s, s + steps) for s in range(first, last)])


def near_docs(doc_ref, tok):
    me = lax.axis_index("ctx")
    last = lax.axis_size("ctx") - 1
    at = lambda i: doc_ref[:, pl.ds(pl.multiple_of(i * tok, tok), tok)]
    before = jnp.where(me > 0, at(jnp.maximum(me - 1, 0)), -1)
    after = jnp.where(me < last, at(jnp.minimum(me + 1, last)), -2)
    return jnp.concatenate([before, at(me), after], axis=1).astype(F32)


def doc_column(row):
    return jnp.broadcast_to(row, (row.shape[1], row.shape[1])).T


def shift_matrix(col, row, steps):
    size = col.shape[0]
    place = lax.broadcasted_iota(jnp.int32, (size, size), 1) - lax.broadcasted_iota(jnp.int32, (size, size), 0)
    return jnp.where((place == steps) & (col == row), 1.0, 0.0).astype(BF)


def mix_kernel(doc_ref, q_ref, k_ref, v_ref, bq_ref, bk_ref, bv_ref, wq_ref, wk_ref, wv_ref, cot_ref,
               q_out, k_out, v_out, prod_ref, gm_ref, shifts, edge):
    tok, chunk = q_ref.shape
    wide = 2 * LANES

    @pl.when(pl.program_id(0) == 0)
    def _():
        docs = near_docs(doc_ref, tok)
        own = docs[:, tok : 2 * tok]
        col = doc_column(own)
        shifts[0:tok, :] = shift_matrix(col, own, -1)
        shifts[tok:, :] = shift_matrix(col, own, -2)
        place = lax.broadcasted_iota(jnp.int32, (8, LANES), 0)
        old = [jnp.broadcast_to(docs[:, tok - d : tok - d + 1], (8, LANES)) for d in (1, 2)]
        first = col[:8, :]
        edge[0] = jnp.where((place == 0) & (first == old[0]), 1.0, 0.0)
        edge[1] = jnp.where((place == 0) & (first == old[1]), 1.0, 0.0)
        edge[2] = jnp.where((place == 1) & (first == old[0]), 1.0, 0.0)

    edges = [jnp.concatenate([edge[i]] * 2, axis=1) for i in range(3)]

    def mixed(x_ref, b_ref, w_ref, out, at):
        x = x_ref[:, at]
        moved = jnp.dot(shifts[...], x, preferred_element_type=F32)
        border = b_ref[:, at].astype(F32)
        w = w_ref[:, at]
        total = w[0:1] * x.astype(F32) + w[1:2] * moved[:tok] + w[2:3] * moved[tok:]
        fix = w[1:2] * (edges[0] * border[1:2]) + w[2:3] * (edges[1] * border[0:1] + edges[2] * border[1:2])
        total = jnp.concatenate([total[:8] + fix, total[8:]], axis=0)
        rounded = total.astype(BF)
        out[:, at] = rounded
        return rounded.astype(F32)

    for i in range(chunk // wide):
        at = slice(i * wide, (i + 1) * wide)
        gm_ref[:, at] = (cot_ref[:, at].astype(F32) * mixed(q_ref, bq_ref, wq_ref, q_out, at)).astype(BF)
        key = mixed(k_ref, bk_ref, wk_ref, k_out, at)
        prod_ref[:, at] = (key * mixed(v_ref, bv_ref, wv_ref, v_out, at)).astype(BF)


def banded(filt, rows):
    parts = []
    for g in range(filt.shape[0]):
        wide = jnp.broadcast_to(filt[g : g + 1, :], (rows, filt.shape[1]))
        parts.append(pltpu.roll(wide, 0, 1, stride=1, stride_axis=0).astype(BF))
    return parts


def diagonal_sums(part, width):
    half = part.shape[0] // 2
    while half >= 8:
        part = part[:half] + pltpu.roll(part[half:], width - half, 1)
        half //= 2
    while half >= 1:
        part = part + pltpu.roll(pltpu.roll(part, 8 - half, 0), width - half, 1)
        half //= 2
    return part[0:1]


def long_kernel(groups, doc_ref, filt_ref, q_ref, k_ref, v_ref, cot_ref, prod_ref, gm_ref,
                before_ref, after_ref, out_ref, mg_ref, gl_ref, keeps, keeps32, pwin, gwin, wide):
    rows = ROWS
    tok, width = q_ref.shape
    steps = tok // rows
    lane_group = lax.broadcasted_iota(jnp.int32, (rows, LANES), 1) // (LANES // groups)

    @pl.when(pl.program_id(0) == 0)
    def _():
        docs = near_docs(doc_ref, tok)
        col = doc_column(docs[:, tok : 2 * tok])
        col = jnp.concatenate([col, col], axis=1)
        row = jnp.concatenate([jnp.broadcast_to(docs, (8, 3 * tok)), jnp.full((8, tok), -3.0, F32)], axis=1)
        for a in range(steps):
            mine = col[a * rows : (a + 1) * rows]
            for b, start in ((a, a * rows), (steps + a, tok + a * rows)):
                window = pltpu.roll(row, (4 * tok - start) % (4 * tok), 1)[0:1, : 2 * tok]
                keep = jnp.where(mine == window, 1.0, 0.0)
                keeps32[b * rows : (b + 1) * rows, :] = keep
                keeps[b * rows : (b + 1) * rows, :] = keep.astype(BF)
        pwin[2 * tok :, :] = jnp.zeros((tok, width), BF)
        gwin[2 * tok :, :] = jnp.zeros((tok, width), BF)

    pwin[0:tok, :] = before_ref[...]
    pwin[tok : 2 * tok, :] = prod_ref[...]
    gwin[0:tok, :] = gm_ref[...]
    gwin[tok : 2 * tok, :] = after_ref[...]
    filt = filt_ref[...]
    total = filt.shape[0]
    turn = lax.broadcasted_iota(jnp.int32, (tok, tok), 0) + lax.broadcasted_iota(jnp.int32, (tok, tok), 1)
    turned = jnp.dot(filt, jnp.where(turn == tok, 1.0, 0.0).astype(BF), preferred_element_type=F32)
    filt = filt.astype(F32)
    lane = lax.broadcasted_iota(jnp.int32, (total, tok), 1)
    wide[:, 0:tok] = turned
    wide[:, tok : 2 * tok] = jnp.where(lane == 0, filt, 0.0)
    wide[:, 2 * tok : 3 * tok] = filt
    wide[:, 3 * tok :] = jnp.zeros((total, tok), F32)

    def pick(value):
        chosen = value[:rows]
        for g in range(1, groups):
            chosen = jnp.where(lane_group == g, value[g * rows : (g + 1) * rows], chosen)
        return chosen

    for i in range(width // LANES):
        at = slice(i * LANES, (i + 1) * LANES)
        own = slice(i * groups, (i + 1) * groups)
        ahead = banded(wide[own, : 2 * tok], rows)
        back = banded(wide[own, 2 * tok :], rows)
        diag = None
        for a in range(steps):
            here = slice(a * rows, (a + 1) * rows)
            there = slice((steps + a) * rows, (steps + a + 1) * rows)
            span = slice(a * rows, a * rows + 2 * tok)
            keep = keeps[here, :]
            mix = jnp.dot(jnp.concatenate([b * keep for b in ahead], axis=0), pwin[span, at], preferred_element_type=F32)
            mix = pick(mix).astype(BF).astype(F32)
            out_ref[here, at] = (q_ref[here, at].astype(F32) * mix).astype(BF)
            mg_ref[0, here, at] = (cot_ref[here, at].astype(F32) * mix).astype(BF)
            keep = keeps[there, :]
            grad = jnp.dot(jnp.concatenate([b * keep for b in back], axis=0), gwin[span, at], preferred_element_type=F32)
            grad = pick(grad).astype(BF).astype(F32)
            mg_ref[1, here, at] = (grad * v_ref[here, at].astype(F32)).astype(BF)
            mg_ref[2, here, at] = (grad * k_ref[here, at].astype(F32)).astype(BF)
            mine = prod_ref[here, at]
            zero = jnp.zeros_like(mine)
            spread = jnp.concatenate([jnp.where(lane_group == g, mine, zero) for g in range(groups)], axis=0)
            pairs = lax.dot_general(spread, gwin[span, at], (((1,), (1,)), ((), ())), preferred_element_type=F32)
            keep = keeps32[there, :]
            pairs = [pairs[g * rows : (g + 1) * rows] * keep for g in range(groups)]
            diag = pairs if diag is None else [x + y for x, y in zip(diag, pairs)]
        gl_ref[own, :] = jnp.concatenate([diagonal_sums(d, 2 * tok)[:, :tok] for d in diag], axis=0)


def close_kernel(doc_ref, mg_ref, next_ref, x_ref, w_ref, out_ref, gs_ref, shifts, edge):
    tok, chunk = x_ref.shape
    wide = 2 * LANES

    @pl.when((pl.program_id(0) == 0) & (pl.program_id(1) == 0))
    def _():
        docs = near_docs(doc_ref, tok)
        own = docs[:, tok : 2 * tok]
        col = doc_column(own)
        shifts[0:tok, :] = shift_matrix(col, own, 1)
        shifts[tok:, :] = shift_matrix(col, own, 2)
        place = lax.broadcasted_iota(jnp.int32, (8, LANES), 0)
        new = [jnp.broadcast_to(docs[:, 2 * tok + d : 2 * tok + d + 1], (8, LANES)) for d in (0, 1)]
        final = col[tok - 8 :, :]
        edge[0] = jnp.where((place == 7) & (final == new[0]), 1.0, 0.0)
        edge[1] = jnp.where((place == 6) & (final == new[0]), 1.0, 0.0)
        edge[2] = jnp.where((place == 7) & (final == new[1]), 1.0, 0.0)

    edges = [jnp.concatenate([edge[i]] * 2, axis=1) for i in range(3)]
    for i in range(chunk // wide):
        at = slice(i * wide, (i + 1) * wide)
        g = mg_ref[0, :, at]
        moved = jnp.dot(shifts[...], g, preferred_element_type=F32)
        border = next_ref[0, :, at].astype(F32)
        one, two = moved[:tok], moved[tok:]
        one = jnp.concatenate([one[: tok - 8], one[tok - 8 :] + edges[0] * border[0:1]], axis=0)
        two = jnp.concatenate([two[: tok - 8], two[tok - 8 :] + edges[1] * border[0:1] + edges[2] * border[1:2]], axis=0)
        g = g.astype(F32)
        w = w_ref[:, at]
        out_ref[:, at] = (w[0:1] * g + w[1:2] * one + w[2:3] * two).astype(BF)
        x = x_ref[:, at].astype(F32)
        for tap, moved_grad in enumerate((g, one, two)):
            gs_ref[tap : tap + 1, at] = jnp.sum(moved_grad * x, axis=0, keepdims=True)


def reduce_kernel(depth, short_ref, long_ref, s_out, l_out, s1, l1, s2, l2, s3, l3, bs, bl, send, recv):
    dp, ctx = lax.axis_index("dp"), lax.axis_index("ctx")
    rows = lax.axis_size("dp")
    z, x, c = ctx // (ACROSS * CORES), (ctx // CORES) % ACROSS, ctx % CORES
    place = lambda zz, xx, cc: (zz * ACROSS + xx) * CORES + cc

    across = [(dp, place(z, (x + d) % ACROSS, c)) for d in range(1, ACROSS)]
    along = [(dp, place((z + d) % depth, x, c)) for d in range(1, depth)]
    final = []
    for d in range(1, rows * CORES):
        final.append(((dp + d // CORES) % rows, place(z, x, (c + d) % CORES)))
    peers = across + along + final
    barrier = pltpu.get_barrier_semaphore()
    for peer in peers:
        pl.semaphore_signal(barrier, inc=1, device_id=peer, device_id_type=MESH)
    pl.semaphore_wait(barrier, len(peers))

    def exchange(targets, sources, slot):
        copies = []
        for i, (peer, pairs) in enumerate(zip(targets, sources)):
            for j, (src, dst) in enumerate(pairs):
                at = 2 * (slot + i) + j
                copies.append(
                    pltpu.make_async_remote_copy(
                        src_ref=src, dst_ref=dst, send_sem=send.at[at], recv_sem=recv.at[at],
                        device_id=peer, device_id_type=MESH,
                    )
                )
        for copy in copies:
            copy.start()
        return copies

    def finish(copies):
        for copy in copies:
            copy.wait_recv()

    def total(first, arrived):
        for i in range(arrived.shape[0]):
            first = first + arrived[i]
        return first

    n1, n2, n3 = len(across), len(along), len(final)
    one = exchange(
        across,
        [
            [(short_ref.at[(x + d) % ACROSS], s1.at[d - 1]), (long_ref.at[(x + d) % ACROSS], l1.at[d - 1])]
            for d in range(1, ACROSS)
        ],
        0,
    )
    finish(one)
    bs[...] = total(short_ref[x], s1)
    bl[...] = total(long_ref[x], l1)
    two = exchange(
        along,
        [
            [(bs.at[(z + d) % depth], s2.at[d - 1]), (bl.at[(z + d) % depth], l2.at[d - 1])]
            for d in range(1, depth)
        ],
        n1,
    )
    finish(two)
    s3[n3] = total(bs[z], s2)
    l3[n3] = total(bl[z], l2)
    three = exchange(final, [[(s3.at[n3], s3.at[d]), (l3.at[n3], l3.at[d])] for d in range(n3)], n1 + n2)
    finish(three)
    s_out[...] = total(s3[n3], s3.at[pl.ds(0, n3)])
    l_out[...] = total(l3[n3], l3.at[pl.ds(0, n3)])
    for copy in one + two + three:
        copy.wait_send()


def mix_call(docs, x, border, w, cot, chunk):
    tok, width = cot.shape
    n = width // chunk
    third = [lambda i, p=p: (0, p * n + i) for p in range(3)]
    flat = lambda i: (0, i)
    shape = jax.ShapeDtypeStruct((tok, width), BF)
    return pl.pallas_call(
        mix_kernel,
        grid=(n,),
        out_shape=[shape] * 5,
        in_specs=[pl.BlockSpec(docs.shape, lambda i: (0, 0))]
        + [pl.BlockSpec((tok, chunk), m) for m in third]
        + [pl.BlockSpec((2, chunk), m) for m in third]
        + [pl.BlockSpec((3, chunk), m) for m in third]
        + [pl.BlockSpec((tok, chunk), flat)],
        out_specs=[pl.BlockSpec((tok, chunk), flat)] * 5,
        scratch_shapes=[pltpu.VMEM((2 * tok, tok), BF), pltpu.VMEM((3, 8, LANES), F32)],
        compiler_params=pltpu.CompilerParams(vmem_limit_bytes=VMEM),
        name="mix",
    )(docs, x, x, x, border, border, border, w, w, w, cot)


def long_call(docs, filt, q, k, v, cot, prod, gm, before, after, chunk):
    tok, width = cot.shape
    per = width // filt.shape[0]
    n = width // chunk
    flat = pl.BlockSpec((tok, chunk), lambda i: (0, i))
    return pl.pallas_call(
        functools.partial(long_kernel, LANES // per),
        grid=(n,),
        out_shape=[
            jax.ShapeDtypeStruct((tok, width), BF),
            jax.ShapeDtypeStruct((3, tok, width), BF),
            jax.ShapeDtypeStruct(filt.shape, F32),
        ],
        in_specs=[
            pl.BlockSpec(docs.shape, lambda i: (0, 0)),
            pl.BlockSpec((chunk // per, tok), lambda i: (i, 0)),
        ]
        + [flat] * 8,
        out_specs=[
            flat,
            pl.BlockSpec((3, tok, chunk), lambda i: (0, 0, i)),
            pl.BlockSpec((chunk // per, tok), lambda i: (i, 0)),
        ],
        scratch_shapes=[
            pltpu.VMEM((2 * tok, 2 * tok), BF),
            pltpu.VMEM((2 * tok, 2 * tok), F32),
            pltpu.VMEM((3 * tok, chunk), BF),
            pltpu.VMEM((3 * tok, chunk), BF),
            pltpu.VMEM((chunk // per, 4 * tok), F32),
        ],
        compiler_params=pltpu.CompilerParams(vmem_limit_bytes=VMEM),
        name="long",
    )(docs, filt, q, k, v, cot, prod, gm, before, after)


def close_call(docs, mg, ahead, x, w, chunk):
    tok, width = x.shape
    n = mg.shape[2] // chunk
    third = lambda p, i: (0, p * n + i)
    return pl.pallas_call(
        close_kernel,
        grid=(3, n),
        out_shape=[jax.ShapeDtypeStruct((tok, width), BF), jax.ShapeDtypeStruct((3, width), F32)],
        in_specs=[
            pl.BlockSpec(docs.shape, lambda p, i: (0, 0)),
            pl.BlockSpec((1, tok, chunk), lambda p, i: (p, 0, i)),
            pl.BlockSpec((1, 2, chunk), lambda p, i: (p, 0, i)),
            pl.BlockSpec((tok, chunk), third),
            pl.BlockSpec((3, chunk), third),
        ],
        out_specs=[pl.BlockSpec((tok, chunk), third), pl.BlockSpec((3, chunk), third)],
        scratch_shapes=[pltpu.VMEM((2 * tok, tok), BF), pltpu.VMEM((3, 8, LANES), F32)],
        compiler_params=pltpu.CompilerParams(vmem_limit_bytes=VMEM),
        name="close",
    )(docs, mg, ahead, x, w)


def reduce_call(gs, gl, dp, ctx):
    depth = ctx // (ACROSS * CORES)
    pair = gs.shape[1] // (ACROSS * depth)
    some = gl.shape[0] // (ACROSS * depth)
    taps = gl.shape[1]
    short = gs.reshape(3, depth, ACROSS, pair).transpose(2, 1, 0, 3)
    long = gl.reshape(depth, ACROSS, some, taps).transpose(1, 0, 2, 3)
    n3 = dp * CORES - 1
    total = (ACROSS - 1) + (depth - 1) + n3
    space = pl.BlockSpec(memory_space=pltpu.VMEM)
    vm = lambda *s: pltpu.VMEM(s, F32)
    return pl.pallas_call(
        functools.partial(reduce_kernel, depth),
        out_shape=[jax.ShapeDtypeStruct((3, pair), F32), jax.ShapeDtypeStruct((some, taps), F32)],
        in_specs=[space] * 2,
        out_specs=[space] * 2,
        scratch_shapes=[
            vm(ACROSS - 1, depth, 3, pair), vm(ACROSS - 1, depth, some, taps),
            vm(depth - 1, 3, pair), vm(depth - 1, some, taps),
            vm(n3 + 1, 3, pair), vm(n3 + 1, some, taps),
            vm(depth, 3, pair), vm(depth, some, taps),
            pltpu.SemaphoreType.DMA((2 * total,)),
            pltpu.SemaphoreType.DMA((2 * total,)),
        ],
        compiler_params=pltpu.CompilerParams(collective_id=0, has_side_effects=True, vmem_limit_bytes=VMEM),
        name="reduce",
    )(short, long)


def local(projected, doc_ids, short_filter, long_filter, cotangent):
    x, cot = projected[0], cotangent[0]
    tok, width = cot.shape
    groups, taps = long_filter.shape
    parts, rows = lax.axis_size("ctx"), lax.axis_size("dp")
    border = passed_along(x[tok - 2 :], "ctx", 1)
    q, k, v, prod, gm = mix_call(doc_ids, x, border, short_filter, cot, 512)
    before = passed_along(prod, "ctx", 1)
    after = passed_along(gm, "ctx", -1)
    out, mg, gl = long_call(doc_ids, long_filter, q, k, v, cot, prod, gm, before, after, 512)
    ahead = passed_along(mg[:, :2], "ctx", -1)
    gx, gs = close_call(doc_ids, mg, ahead, x, short_filter, 1024)
    gs, gl = reduce_call(gs, gl, rows, parts)
    core = lax.axis_index("ctx") % CORES
    gs = lax.dynamic_slice_in_dim(gs, core * (gs.shape[1] // CORES), gs.shape[1] // CORES, 1)
    gl = lax.dynamic_slice_in_dim(gl, core * (gl.shape[0] // CORES), gl.shape[0] // CORES, 0)
    norm = rows * doc_ids.shape[1]
    return out[None], gx[None], gs / math.sqrt(norm), gl / math.sqrt(norm * (width // groups))


def solution(mesh):
    return jax.shard_map(
        local,
        mesh=mesh,
        in_specs=(P("dp", "ctx", None), P("dp", None), P(), P(), P("dp", "ctx", None)),
        out_specs=(P("dp", "ctx", None), P("dp", "ctx", None), P(None, "ctx"), P("ctx", None)),
        check_vma=False,
    )
```

time: 315 us -> 115 us (0.37)
  waiting for transfers between devices: 202 us -> 17.5 us
  Pallas kernels: 59.5 us -> 73.7 us
  between operations: 14.2 us -> 0.71 us
  blocking collectives: 8.54 us -> 0 us
  local copies, waits for them, and re-layouts: 12.8 us -> 7.63 us
    unnamed x2 -> x0, waiting for transfers between devices: 187 us -> none
    pallas_call x0 -> x1, Pallas kernels: none -> 32.7 us  [reduce_call(): pl.pallas_call(functools.partial(reduce_kernel, depth), out_shape=[jax.Sh...]
    pallas_call x1, Pallas kernels: 34.1 us -> 21.3 us  [long_call(): pl.pallas_call(functools.partial(long_kernel, LANES // per), grid=(n,), o...]
    psum x1 -> x0, blocking collectives: 8.54 us -> none  [local(): lax.psum(lax.psum_scatter(packed, 'ctx', scatter_dimension=0, tiled=True)...]
    pallas_call x1, Pallas kernels: 16.8 us -> 10.6 us  [close_call(): pl.pallas_call(close_kernel, grid=(3, n), out_shape=[jax.ShapeDtypeStruct...]
    unnamed x20 -> x8, local copies, waits for them, and re-layouts: 7.68 us -> 2.3 us
  transfers between devices with their start and end apart: 5 -> 4, of which waited for: 5 -> 4; matrix products, arithmetic and copies ran while one was open for 1% -> 1% of each run, Pallas kernels for 0% -> 0%
where the time goes in v1:
time: 115 us
  Pallas kernels  73.7 us (64%)
  waiting for transfers between devices  17.5 us (15%)
  starting transfers between devices  12.6 us (11%)
  local copies, waits for them, and re-layouts  7.63 us (7%)
  other arithmetic  2.6 us (2%)
    pallas_call x1, Pallas kernels, reduce_call(): pl.pallas_call(functools.partial(reduce_kernel, depth), out_shape=[jax.Sh...  32.7 us
    pallas_call x1, Pallas kernels, long_call(): pl.pallas_call(functools.partial(long_kernel, LANES // per), grid=(n,), o...  21.3 us
    ppermute x4, waiting for transfers between devices, passed_along(): lax.ppermute(value, axis, [(s, s + steps) for s in range(first, last)])  17.5 us
    ppermute x4, starting transfers between devices, passed_along(): lax.ppermute(value, axis, [(s, s + steps) for s in range(first, last)])  12.6 us
    pallas_call x1, Pallas kernels, close_call(): pl.pallas_call(close_kernel, grid=(3, n), out_shape=[jax.ShapeDtypeStruct...  10.6 us
    pallas_call x1, Pallas kernels, mix_call(): pl.pallas_call(mix_kernel, grid=(n,), out_shape=[shape] * 5, in_specs=[pl...  9.05 us
  transfers between devices with their start and end apart: 4, of which 4 were waited for; matrix products, arithmetic and copies ran while one was open for 1% of the time, Pallas kernels for 0%

profile of v1, /device:TPU:1, one launch (start us, length us, event | category | flops | bytes accessed | tf_op | source)
XLA Modules:
  0.0 114.7 jit_solution(5596483281332049481)
XLA Ops:
  0.6 1.0 slice_bitcast_fusion
  1.6 4.5 %collective-permute-start = (bf16[2,12288]{1,0:T(2,128)(2,1)S(1)}, bf16[2,12288]{1,0:T(2,128)(2,1)S(1)}, u32[]{:S(2)}, u32[]{:S(2)}) collective-permute-start(bf16[2,12288]{1,0:T(2,128)(2,1)S(1)} %slice_bitcast_fusion), channel_id=1, source_target_pairs={{0,1},{1,2},{2,3},{3,4},{4,5},{5,6},{6,7},{7,8},{8,9},{9,10},{10,1... | collective-permute-start | bytes 147464 | tf_op jit(solution)/shard_map/ppermute | solution.py:24
  6.1 1.2 %collective-permute-done.bq_ref.bk_ref.bv_ref = bf16[2,12288]{1,0:T(2,128)(2,1)S(1)} collective-permute-done((bf16[2,12288]{1,0:T(2,128)(2,1)S(1)}, bf16[2,12288]{1,0:T(2,128)(2,1)S(1)}, u32[]{:S(2)}, u32[]{:S(2)}) %collective-permute-start) | collective-permute-done | bytes 49184 | tf_op jit(solution)/shard_map/ppermute | solution.py:24
  7.3 0.0 copy-start.2
  7.3 0.6 copy-done.2
  7.9 9.1 %mix.1 = (bf16[128,4096]{1,0:T(8,128)(2,1)}, bf16[128,4096]{1,0:T(8,128)(2,1)}, bf16[128,4096]{1,0:T(8,128)(2,1)}, bf16[128,4096]{1,0:T(8,128)(2,1)}, bf16[128,4096]{1,0:T(8,128)(2,1)}) custom-call(s32[1,8192]{1,0:T(1,128)} %doc_ref.5, bf16[128,12288]{1,0:T(8,128)(2,1)} %bitcast.13, bf16[128,12288]{1,0:T(8,128)(2,1)} %bitcast.14, ...), custom_call_target="tpu_custom_call" | custom-call | tf_op jit(solution)/shard_map/mix/pallas_call | solution.py:292
  17.0 4.2 %collective-permute-start.1 = (bf16[128,4096]{1,0:T(8,128)(2,1)}, bf16[128,4096]{1,0:T(8,128)(2,1)S(1)}, u32[]{:S(2)}, u32[]{:S(2)}) collective-permute-start(bf16[128,4096]{1,0:T(8,128)(2,1)} %get-tuple-element.19.prod_ref), channel_id=1, source_target_pairs={{0,1},{1,2},{2,3},{3,4},{4,5},{5,6},{6,7},{7,8},{8,9},{9,10},{10,1... | collective-permute-start | bytes 3145736 | tf_op jit(solution)/shard_map/ppermute | solution.py:24
  21.2 1.9 %collective-permute-start.2 = (bf16[128,4096]{1,0:T(8,128)(2,1)}, bf16[128,4096]{1,0:T(8,128)(2,1)S(1)}, u32[]{:S(2)}, u32[]{:S(2)}) collective-permute-start(bf16[128,4096]{1,0:T(8,128)(2,1)} %get-tuple-element.20.gm_ref), channel_id=1, source_target_pairs={{1,0},{2,1},{3,2},{4,3},{5,4},{6,5},{7,6},{8,7},{9,8},{10,9},{11,1... | collective-permute-start | bytes 3145736 | tf_op jit(solution)/shard_map/ppermute | solution.py:24
  23.1 10.1 %collective-permute-done.1.before_ref = bf16[128,4096]{1,0:T(8,128)(2,1)S(1)} collective-permute-done((bf16[128,4096]{1,0:T(8,128)(2,1)}, bf16[128,4096]{1,0:T(8,128)(2,1)S(1)}, u32[]{:S(2)}, u32[]{:S(2)}) %collective-permute-start.1) | collective-permute-done | bytes 1048608 | tf_op jit(solution)/shard_map/ppermute | solution.py:24
  33.3 0.0 copy-start
  33.3 4.3 %collective-permute-done.2.after_ref = bf16[128,4096]{1,0:T(8,128)(2,1)S(1)} collective-permute-done((bf16[128,4096]{1,0:T(8,128)(2,1)}, bf16[128,4096]{1,0:T(8,128)(2,1)S(1)}, u32[]{:S(2)}, u32[]{:S(2)}) %collective-permute-start.2) | collective-permute-done | bytes 1048608 | tf_op jit(solution)/shard_map/ppermute | solution.py:24
  37.5 0.0 copy-start.1
  37.6 0.0 copy-done
  37.6 1.1 copy-done.1
  38.6 21.3 %long.1 = (bf16[128,4096]{1,0:T(8,128)(2,1)}, bf16[3,128,4096]{2,1,0:T(8,128)(2,1)}, f32[256,128]{1,0:T(8,128)}) custom-call(s32[1,8192]{1,0:T(1,128)} %doc_ref.5, bf16[256,128]{1,0:T(8,128)(2,1)} %filt_ref.1, bf16[128,4096]{1,0:T(8,128)(2,1)} %get-tuple-element.16.q_ref, bf16[128,4096]{1,0:T(8,128)(2,1)} %get-tuple-element.17.k_ref, ...), custom_call_target="tpu_custom_call" | custom-call | tf_op jit(solution)/shard_map/long/pallas_call | solution.py:313
  59.9 1.0 slice.11
  60.9 1.9 %collective-permute-start.3 = (bf16[3,2,4096]{2,1,0:T(2,128)(2,1)S(1)}, bf16[3,2,4096]{2,1,0:T(2,128)(2,1)S(1)}, u32[]{:S(2)}, u32[]{:S(2)}) collective-permute-start(bf16[3,2,4096]{2,1,0:T(2,128)(2,1)S(1)} %slice.11), channel_id=1, source_target_pairs={{1,0},{2,1},{3,2},{4,3},{5,4},{6,5},{7,6},{8,7},{9,8},{10,9},{11,1... | collective-permute-start | bytes 147464 | tf_op jit(solution)/shard_map/ppermute | solution.py:24
  62.8 1.6 %copy.14 = f32[8,4,8,128]{3,2,0,1:T(8,128)} copy(f32[8,4,8,128]{3,2,1,0:T(8,128)} %bitcast.21) | data formatting | bytes 262144 | tf_op jit(solution)/shard_map/reshape | solution.py:371
  64.4 1.9 %collective-permute-done.3.next_ref = bf16[3,2,4096]{2,1,0:T(2,128)(2,1)S(1)} collective-permute-done((bf16[3,2,4096]{2,1,0:T(2,128)(2,1)S(1)}, bf16[3,2,4096]{2,1,0:T(2,128)(2,1)S(1)}, u32[]{:S(2)}, u32[]{:S(2)}) %collective-permute-start.3) | collective-permute-done | bytes 49184 | tf_op jit(solution)/shard_map/ppermute | solution.py:24
  66.3 0.0 copy-start.3
  66.3 0.6 copy-done.3
  66.9 10.6 %close.1 = (bf16[128,12288]{1,0:T(8,128)(2,1)}, f32[3,12288]{1,0:T(4,128)}) custom-call(s32[1,8192]{1,0:T(1,128)} %doc_ref.5, bf16[3,128,4096]{2,1,0:T(8,128)(2,1)} %get-tuple-element.22.mg_ref, bf16[3,2,4096]{2,1,0:T(2,128)(2,1)} %copy-done.3, bf16[128,12288]{1,0:T(8,128)(2,1)} %bitcast.16, f32[3,12288]{1,0:T(4,128)} %w_ref.1), custom_call_target="tpu_custom_call" | custom-call | tf_op jit(solution)/shard_map/close/pallas_call | solution.py:347
  77.5 1.1 reshape.15
  78.6 0.8 copy.13
  79.3 32.7 %reduce.1 = (f32[3,384]{1,0:T(4,128)}, f32[8,128]{1,0:T(8,128)}) custom-call(f32[4,8,3,384]{3,2,1,0:T(4,128)} %bitcast.19, f32[4,8,8,128]{3,2,1,0:T(8,128)} %bitcast.20), custom_call_target="tpu_custom_call" | custom-call | tf_op jit(solution)/shard_map/reduce/pallas_call | solution.py:376
  112.1 1.3 %dynamic-slice_multiply_fusion.1 = f32[4,128]{1,0:T(4,128)} fusion(f32[8,128]{1,0:T(8,128)} %get-tuple-element.27, s32[]{:T(128)S(6)} %select_n.15), kind=kLoop, calls=%fused_computation.4 | loop fusion | flops 512 | bytes 4100 | tf_op jit(solution)/shard_map/div | solution.py:411
  113.3 1.3 %dynamic-slice_multiply_fusion = f32[3,192]{1,0:T(4,128)} fusion(f32[3,384]{1,0:T(4,128)} %get-tuple-element.26, s32[]{:T(128)S(6)} %select_n.14), kind=kLoop, calls=%fused_computation.3 | loop fusion | flops 576 | bytes 4612 | tf_op jit(solution)/shard_map/div | solution.py:411
Async XLA Ops:
  1.6 5.7 %collective-permute-start = (bf16[2,12288]{1,0:T(2,128)(2,1)S(1)}, bf16[2,12288]{1,0:T(2,128)(2,1)S(1)}, u32[]{:S(2)}, u32[]{:S(2)}) collective-permute-start(bf16[2,12288]{1,0:T(2,128)(2,1)S(1)} %slice_bitcast_fusion), channel_id=1, source_target_pairs={{0,1},{1,2},{2,3},{3,4},{4,5},{5,6},{6,7},{7,8},{8,9},{9,10},{10,1... | collective-permute-start | bytes 147464 | tf_op jit(solution)/shard_map/ppermute | solution.py:24
  7.3 0.6 copy-start.2
  17.0 16.3 %collective-permute-start.1 = (bf16[128,4096]{1,0:T(8,128)(2,1)}, bf16[128,4096]{1,0:T(8,128)(2,1)S(1)}, u32[]{:S(2)}, u32[]{:S(2)}) collective-permute-start(bf16[128,4096]{1,0:T(8,128)(2,1)} %get-tuple-element.19.prod_ref), channel_id=1, source_target_pairs={{0,1},{1,2},{2,3},{3,4},{4,5},{5,6},{6,7},{7,8},{8,9},{9,10},{10,1... | collective-permute-start | bytes 3145736 | tf_op jit(solution)/shard_map/ppermute | solution.py:24
  21.2 16.3 %collective-permute-start.2 = (bf16[128,4096]{1,0:T(8,128)(2,1)}, bf16[128,4096]{1,0:T(8,128)(2,1)S(1)}, u32[]{:S(2)}, u32[]{:S(2)}) collective-permute-start(bf16[128,4096]{1,0:T(8,128)(2,1)} %get-tuple-element.20.gm_ref), channel_id=1, source_target_pairs={{1,0},{2,1},{3,2},{4,3},{5,4},{6,5},{7,6},{8,7},{9,8},{10,9},{11,1... | collective-permute-start | bytes 3145736 | tf_op jit(solution)/shard_map/ppermute | solution.py:24
  33.3 4.3 %copy-start = (bf16[128,4096]{1,0:T(8,128)(2,1)}, bf16[128,4096]{1,0:T(8,128)(2,1)S(1)}, u32[]{:S(2)}) copy-start(bf16[128,4096]{1,0:T(8,128)(2,1)S(1)} %collective-permute-done.1.before_ref) | copy-start | bytes 3145732
  37.5 1.1 copy-start.1
  60.9 5.4 %collective-permute-start.3 = (bf16[3,2,4096]{2,1,0:T(2,128)(2,1)S(1)}, bf16[3,2,4096]{2,1,0:T(2,128)(2,1)S(1)}, u32[]{:S(2)}, u32[]{:S(2)}) collective-permute-start(bf16[3,2,4096]{2,1,0:T(2,128)(2,1)S(1)} %slice.11), channel_id=1, source_target_pairs={{1,0},{2,1},{3,2},{4,3},{5,4},{6,5},{7,6},{8,7},{9,8},{10,9},{11,1... | collective-permute-start | bytes 147464 | tf_op jit(solution)/shard_map/ppermute | solution.py:24
  66.3 0.6 copy-start.3

commit v2 on v1

v2 whole, which is shorter than its diff:
```python
import functools
import math

import jax
import jax.numpy as jnp
from jax import lax
from jax.experimental import pallas as pl
from jax.experimental.pallas import tpu as pltpu
from jax.sharding import PartitionSpec as P

BF = jnp.bfloat16
F32 = jnp.float32
MESH = pl.DeviceIdType.MESH
ROWS = 16
LANES = 128
CORES = 2
ACROSS = 4
VMEM = 56 << 20


def near_docs(doc_ref, tok):
    me = lax.axis_index("ctx")
    last = lax.axis_size("ctx") - 1
    at = lambda i: doc_ref[:, pl.ds(pl.multiple_of(i * tok, tok), tok)]
    before = jnp.where(me > 0, at(jnp.maximum(me - 1, 0)), -1)
    after = jnp.where(me < last, at(jnp.minimum(me + 1, last)), -2)
    return jnp.concatenate([before, at(me), after], axis=1).astype(F32)


def doc_column(row):
    return jnp.broadcast_to(row, (row.shape[1], row.shape[1])).T


def shift_matrix(col, row, steps):
    size = col.shape[0]
    place = lax.broadcasted_iota(jnp.int32, (size, size), 1) - lax.broadcasted_iota(jnp.int32, (size, size), 0)
    return jnp.where((place == steps) & (col == row), 1.0, 0.0).astype(BF)


def ring(steps):
    size = lax.axis_size("ctx")
    return lax.axis_index("dp"), (lax.axis_index("ctx") + size + steps) % size


def greet(peers):
    barrier = pltpu.get_barrier_semaphore()
    for peer in peers:
        pl.semaphore_signal(barrier, inc=1, device_id=peer, device_id_type=MESH)
    pl.semaphore_wait(barrier, len(peers))


def sent(src, dst, send, recv, peer):
    return pltpu.make_async_remote_copy(
        src_ref=src, dst_ref=dst, send_sem=send, recv_sem=recv, device_id=peer, device_id_type=MESH
    )


def mix_kernel(chunk, doc_ref, w_ref, x_hbm, cot_hbm, q_out, k_out, v_out, prod_out, gm_out, before_out, after_out,
               xs, cs, tail, mine, border, qs, ks, vs, ps, gs, shifts, edge,
               tail_sem, in_sem, out_sem, edge_sem, send, recv):
    tok, width = cs.shape
    wide = 2 * LANES
    count = width // chunk
    right, left = ring(1), ring(-1)

    def at(i, size=chunk, offset=0):
        return pl.ds(pl.multiple_of(offset + i * size, LANES), size)

    def loads(i):
        for p in range(3):
            here = at(i, offset=p * width)
            yield pltpu.make_async_copy(x_hbm.at[:, here], xs.at[:, here], in_sem.at[p, i])
        yield pltpu.make_async_copy(cot_hbm.at[:, at(i)], cs.at[:, at(i)], in_sem.at[3, i])

    def saves(i):
        pairs = ((qs, q_out), (ks, k_out), (vs, v_out), (ps, prod_out), (gs, gm_out))
        for p, (src, dst) in enumerate(pairs):
            yield pltpu.make_async_copy(src.at[:, at(i)], dst.at[:, at(i)], out_sem.at[p, i])

    def sends(i):
        yield sent(ps.at[:, at(i)], before_out.at[:, at(i)], send.at[0, i], recv.at[0, i], right)
        yield sent(gs.at[:, at(i)], after_out.at[:, at(i)], send.at[1, i], recv.at[1, i], left)

    first = pltpu.make_async_copy(x_hbm.at[tok - 16 :, :], tail, tail_sem)
    first.start()
    for i in range(count):
        for copy in loads(i):
            copy.start()
    docs = near_docs(doc_ref, tok)
    own = docs[:, tok : 2 * tok]
    col = doc_column(own)
    shifts[0:tok, :] = shift_matrix(col, own, -1)
    shifts[tok:, :] = shift_matrix(col, own, -2)
    place = lax.broadcasted_iota(jnp.int32, (8, LANES), 0)
    old = [jnp.broadcast_to(docs[:, tok - d : tok - d + 1], (8, LANES)) for d in (1, 2)]
    head = col[:8, :]
    edge[0] = jnp.where((place == 0) & (head == old[0]), 1.0, 0.0)
    edge[1] = jnp.where((place == 0) & (head == old[1]), 1.0, 0.0)
    edge[2] = jnp.where((place == 1) & (head == old[0]), 1.0, 0.0)
    first.wait()
    mine[...] = tail[14:16, :]
    greet([right, left])
    edge_copy = sent(mine, border, edge_sem.at[0], edge_sem.at[1], right)
    edge_copy.start()
    edge_copy.wait()

    def mixed(i, j, part):
        here = pl.ds(pl.multiple_of(part * width + i * chunk + j * wide, LANES), wide)
        edges = [jnp.concatenate([edge[n]] * 2, axis=1) for n in range(3)]
        x = xs[:, here]
        moved = jnp.dot(shifts[...], x, preferred_element_type=F32)
        side = border[:, here].astype(F32)
        w = w_ref[:, here]
        total = w[0:1] * x.astype(F32) + w[1:2] * moved[:tok] + w[2:3] * moved[tok:]
        fix = w[1:2] * (edges[0] * side[1:2]) + w[2:3] * (edges[1] * side[0:1] + edges[2] * side[1:2])
        return jnp.concatenate([total[:8] + fix, total[8:]], axis=0).astype(BF)

    def step(i, carry):
        for copy in loads(i):
            copy.wait()
        for j in range(chunk // wide):
            here = pl.ds(pl.multiple_of(i * chunk + j * wide, LANES), wide)
            q, k, v = mixed(i, j, 0), mixed(i, j, 1), mixed(i, j, 2)
            qs[:, here], ks[:, here], vs[:, here] = q, k, v
            gs[:, here] = (cs[:, here].astype(F32) * q.astype(F32)).astype(BF)
            ps[:, here] = (k.astype(F32) * v.astype(F32)).astype(BF)
        for copy in sends(i):
            copy.start()
        for copy in saves(i):
            copy.start()
        return carry

    lax.fori_loop(0, count, step, 0)

    def drain(i, carry):
        for copy in saves(i):
            copy.wait()
        for copy in sends(i):
            copy.wait()
        return carry

    lax.fori_loop(0, count, drain, 0)


def banded(filt, rows):
    parts = []
    for g in range(filt.shape[0]):
        wide = jnp.broadcast_to(filt[g : g + 1, :], (rows, filt.shape[1]))
        parts.append(pltpu.roll(wide, 0, 1, stride=1, stride_axis=0).astype(BF))
    return parts


def diagonal_sums(part, width):
    half = part.shape[0] // 2
    while half >= 8:
        part = part[:half] + pltpu.roll(part[half:], width - half, 1)
        half //= 2
    while half >= 1:
        part = part + pltpu.roll(pltpu.roll(part, 8 - half, 0), width - half, 1)
        half //= 2
    return part[0:1]


def long_kernel(groups, doc_ref, filt_ref, q_ref, k_ref, v_ref, cot_ref, prod_ref, gm_ref,
                before_ref, after_ref, out_ref, mg_ref, gl_ref, keeps, keeps32, pwin, gwin, wide):
    rows = ROWS
    tok, width = q_ref.shape
    steps = tok // rows
    lane_group = lax.broadcasted_iota(jnp.int32, (rows, LANES), 1) // (LANES // groups)

    @pl.when(pl.program_id(0) == 0)
    def _():
        docs = near_docs(doc_ref, tok)
        col = doc_column(docs[:, tok : 2 * tok])
        col = jnp.concatenate([col, col], axis=1)
        row = jnp.concatenate([jnp.broadcast_to(docs, (8, 3 * tok)), jnp.full((8, tok), -3.0, F32)], axis=1)
        for a in range(steps):
            mine = col[a * rows : (a + 1) * rows]
            for b, start in ((a, a * rows), (steps + a, tok + a * rows)):
                window = pltpu.roll(row, (4 * tok - start) % (4 * tok), 1)[0:1, : 2 * tok]
                keep = jnp.where(mine == window, 1.0, 0.0)
                keeps32[b * rows : (b + 1) * rows, :] = keep
                keeps[b * rows : (b + 1) * rows, :] = keep.astype(BF)
        pwin[2 * tok :, :] = jnp.zeros((tok, width), BF)
        gwin[2 * tok :, :] = jnp.zeros((tok, width), BF)

    pwin[0:tok, :] = before_ref[...]
    pwin[tok : 2 * tok, :] = prod_ref[...]
    gwin[0:tok, :] = gm_ref[...]
    gwin[tok : 2 * tok, :] = after_ref[...]
    filt = filt_ref[...]
    total = filt.shape[0]
    turn = lax.broadcasted_iota(jnp.int32, (tok, tok), 0) + lax.broadcasted_iota(jnp.int32, (tok, tok), 1)
    turned = jnp.dot(filt, jnp.where(turn == tok, 1.0, 0.0).astype(BF), preferred_element_type=F32)
    filt = filt.astype(F32)
    lane = lax.broadcasted_iota(jnp.int32, (total, tok), 1)
    wide[:, 0:tok] = turned
    wide[:, tok : 2 * tok] = jnp.where(lane == 0, filt, 0.0)
    wide[:, 2 * tok : 3 * tok] = filt
    wide[:, 3 * tok :] = jnp.zeros((total, tok), F32)

    def pick(value):
        chosen = value[:rows]
        for g in range(1, groups):
            chosen = jnp.where(lane_group == g, value[g * rows : (g + 1) * rows], chosen)
        return chosen

    for i in range(width // LANES):
        at = slice(i * LANES, (i + 1) * LANES)
        own = slice(i * groups, (i + 1) * groups)
        ahead = banded(wide[own, : 2 * tok], rows)
        back = banded(wide[own, 2 * tok :], rows)
        diag = None
        for a in range(steps):
            here = slice(a * rows, (a + 1) * rows)
            there = slice((steps + a) * rows, (steps + a + 1) * rows)
            span = slice(a * rows, a * rows + 2 * tok)
            keep = keeps[here, :]
            mix = jnp.dot(jnp.concatenate([b * keep for b in ahead], axis=0), pwin[span, at], preferred_element_type=F32)
            mix = pick(mix).astype(BF).astype(F32)
            out_ref[here, at] = (q_ref[here, at].astype(F32) * mix).astype(BF)
            mg_ref[0, here, at] = (cot_ref[here, at].astype(F32) * mix).astype(BF)
            keep = keeps[there, :]
            grad = jnp.dot(jnp.concatenate([b * keep for b in back], axis=0), gwin[span, at], preferred_element_type=F32)
            grad = pick(grad).astype(BF).astype(F32)
            mg_ref[1, here, at] = (grad * v_ref[here, at].astype(F32)).astype(BF)
            mg_ref[2, here, at] = (grad * k_ref[here, at].astype(F32)).astype(BF)
            mine = prod_ref[here, at]
            zero = jnp.zeros_like(mine)
            spread = jnp.concatenate([jnp.where(lane_group == g, mine, zero) for g in range(groups)], axis=0)
            pairs = lax.dot_general(spread, gwin[span, at], (((1,), (1,)), ((), ())), preferred_element_type=F32)
            keep = keeps32[there, :]
            pairs = [pairs[g * rows : (g + 1) * rows] * keep for g in range(groups)]
            diag = pairs if diag is None else [x + y for x, y in zip(diag, pairs)]
        gl_ref[own, :] = jnp.concatenate([diagonal_sums(d, 2 * tok)[:, :tok] for d in diag], axis=0)


def close_kernel(depth, piece, doc_ref, w_ref, long_ref, mg_hbm, x_hbm, gx_out, s_out, l_out,
                 xs, gs, ys, heads, mine, ahead, shifts, edge, sums,
                 s1, l1, s2, l2, s3, l3, bs, bl, head_sem, g_sem, x_sem, y_sem, row_sem, send, recv):
    tok, full = xs.shape
    width = full // 3
    chunk = full // depth
    pair = chunk // ACROSS
    dp, ctx = lax.axis_index("dp"), lax.axis_index("ctx")
    rows = lax.axis_size("dp")
    z, x, c = ctx // (ACROSS * CORES), (ctx // CORES) % ACROSS, ctx % CORES
    place = lambda zz, xx, cc: (zz * ACROSS + xx) * CORES + cc
    across = [(dp, place(z, (x + d) % ACROSS, c)) for d in range(1, ACROSS)]
    along = [(dp, place((z + d) % depth, x, c)) for d in range(1, depth)]
    final = [((dp + d // CORES) % rows, place(z, x, (c + d) % CORES)) for d in range(1, rows * CORES)]
    n1, n2, n3 = len(across), len(along), len(final)
    right, left = ring(1), ring(-1)

    def flat(i, size):
        return pl.ds(pl.multiple_of(i * size, LANES), size)

    per = width // piece

    def g_load(n):
        src = mg_hbm.at[n // per, :, flat(n % per, piece)]
        return pltpu.make_async_copy(src, gs.at[:, flat(n, piece)], g_sem.at[n])

    def x_load(i):
        return pltpu.make_async_copy(x_hbm.at[:, flat(i, chunk)], xs.at[:, flat(i, chunk)], x_sem.at[i])

    def y_save(i):
        return pltpu.make_async_copy(ys.at[:, flat(i, chunk)], gx_out.at[:, flat(i, chunk)], y_sem.at[i])

    def first_exchange(src, dst, k):
        return [sent(src.at[(x + d) % ACROSS], dst.at[d - 1], send.at[k, d - 1], recv.at[k, d - 1], across[d - 1])
                for d in range(1, ACROSS)]

    def second_exchange(src, dst, k):
        return [sent(src.at[(z + d) % depth], dst.at[d - 1], send.at[k, n1 + d - 1], recv.at[k, n1 + d - 1], along[d - 1])
                for d in range(1, depth)]

    def third_exchange(buf, k):
        return [sent(buf.at[n3], buf.at[d], send.at[k, n1 + n2 + d], recv.at[k, n1 + n2 + d], final[d])
                for d in range(n3)]

    def begin(copies):
        for copy in copies:
            copy.start()

    def arrive(copies):
        for copy in copies:
            copy.wait_recv()

    def total(start, arrived, n):
        for i in range(n):
            start = start + arrived[i]
        return start

    head = pltpu.make_async_copy(mg_hbm.at[:, 0:16, :], heads, head_sem)
    head.start()
    for i in range(depth):
        x_load(i).start()
        for n in range(i * chunk // piece, (i + 1) * chunk // piece):
            g_load(n).start()
    docs = near_docs(doc_ref, tok)
    own = docs[:, tok : 2 * tok]
    col = doc_column(own)
    shifts[0:tok, :] = shift_matrix(col, own, 1)
    shifts[tok:, :] = shift_matrix(col, own, 2)
    row = lax.broadcasted_iota(jnp.int32, (8, LANES), 0)
    new = [jnp.broadcast_to(docs[:, 2 * tok + d : 2 * tok + d + 1], (8, LANES)) for d in (0, 1)]
    end = col[tok - 8 :, :]
    edge[0] = jnp.where((row == 7) & (end == new[0]), 1.0, 0.0)
    edge[1] = jnp.where((row == 6) & (end == new[0]), 1.0, 0.0)
    edge[2] = jnp.where((row == 7) & (end == new[1]), 1.0, 0.0)
    head.wait()
    for p in range(3):
        mine[:, p * width : (p + 1) * width] = heads[p, 0:2, :]
    greet([right, left] + across + along + final)
    row_copy = sent(mine, ahead, row_sem.at[0], row_sem.at[1], left)
    row_copy.start()
    long_one = first_exchange(long_ref, l1, 1)
    begin(long_one)
    row_copy.wait()

    def step(i, carry):
        x_load(i).wait()
        for n in range(chunk // piece):
            g_load(i * (chunk // piece) + n).wait()
        edges = [jnp.concatenate([edge[n]] * (pair // LANES), axis=1) for n in range(3)]
        for j in range(ACROSS):
            here = pl.ds(pl.multiple_of(i * chunk + j * pair, LANES), pair)
            g = gs[:, here]
            moved = jnp.dot(shifts[...], g, preferred_element_type=F32)
            side = ahead[:, here].astype(F32)
            one, two = moved[:tok], moved[tok:]
            one = jnp.concatenate([one[: tok - 8], one[tok - 8 :] + edges[0] * side[0:1]], axis=0)
            two = jnp.concatenate(
                [two[: tok - 8], two[tok - 8 :] + edges[1] * side[0:1] + edges[2] * side[1:2]], axis=0
            )
            g = g.astype(F32)
            w = w_ref[:, here]
            ys[:, here] = (w[0:1] * g + w[1:2] * one + w[2:3] * two).astype(BF)
            source = xs[:, here].astype(F32)
            sums[j, i] = jnp.concatenate(
                [jnp.sum(moved_grad * source, axis=0, keepdims=True) for moved_grad in (g, one, two)], axis=0
            )
        y_save(i).start()
        return carry

    half = depth // 2
    lax.fori_loop(0, half, step, 0)
    arrive(long_one)
    bl[...] = total(long_ref[x], l1, n1)
    long_two = second_exchange(bl, l2, 1)
    begin(long_two)
    lax.fori_loop(half, depth, step, 0)
    short_one = first_exchange(sums, s1, 0)
    begin(short_one)
    arrive(long_two)
    l3[n3] = total(bl[z], l2, n2)
    long_three = third_exchange(l3, 1)
    begin(long_three)
    arrive(short_one)
    bs[...] = total(sums[x], s1, n1)
    short_two = second_exchange(bs, s2, 0)
    begin(short_two)
    arrive(long_three)
    l_out[...] = total(l3[n3], l3, n3)
    arrive(short_two)
    s3[n3] = total(bs[z], s2, n2)
    short_three = third_exchange(s3, 0)
    begin(short_three)
    for i in range(depth):
        y_save(i).wait()
    arrive(short_three)
    s_out[...] = total(s3[n3], s3, n3)
    for copy in long_one + long_two + long_three + short_one + short_two + short_three:
        copy.wait_send()


def mix_call(docs, x, w, cot, chunk):
    tok, width = cot.shape
    n = width // chunk
    shape = jax.ShapeDtypeStruct((tok, width), BF)
    space, far = pl.BlockSpec(memory_space=pltpu.VMEM), pl.BlockSpec(memory_space=pl.ANY)
    dma = pltpu.SemaphoreType.DMA
    return pl.pallas_call(
        functools.partial(mix_kernel, chunk),
        out_shape=[shape] * 7,
        in_specs=[space, space, far, far],
        out_specs=[far] * 7,
        scratch_shapes=[
            pltpu.VMEM((tok, 3 * width), BF), pltpu.VMEM((tok, width), BF), pltpu.VMEM((16, 3 * width), BF),
            pltpu.VMEM((2, 3 * width), BF), pltpu.VMEM((2, 3 * width), BF),
        ]
        + [pltpu.VMEM((tok, width), BF)] * 5
        + [
            pltpu.VMEM((2 * tok, tok), BF), pltpu.VMEM((3, 8, LANES), F32),
            dma, dma((4, n)), dma((5, n)), dma((2,)), dma((2, n)), dma((2, n)),
        ],
        compiler_params=pltpu.CompilerParams(collective_id=0, has_side_effects=True, vmem_limit_bytes=VMEM),
        name="mix",
    )(docs, w, x, cot)


def long_call(docs, filt, q, k, v, cot, prod, gm, before, after, chunk):
    tok, width = cot.shape
    per = width // filt.shape[0]
    n = width // chunk
    flat = pl.BlockSpec((tok, chunk), lambda i: (0, i))
    return pl.pallas_call(
        functools.partial(long_kernel, LANES // per),
        grid=(n,),
        out_shape=[
            jax.ShapeDtypeStruct((tok, width), BF),
            jax.ShapeDtypeStruct((3, tok, width), BF),
            jax.ShapeDtypeStruct(filt.shape, F32),
        ],
        in_specs=[
            pl.BlockSpec(docs.shape, lambda i: (0, 0)),
            pl.BlockSpec((chunk // per, tok), lambda i: (i, 0)),
        ]
        + [flat] * 8,
        out_specs=[
            flat,
            pl.BlockSpec((3, tok, chunk), lambda i: (0, 0, i)),
            pl.BlockSpec((chunk // per, tok), lambda i: (i, 0)),
        ],
        scratch_shapes=[
            pltpu.VMEM((2 * tok, 2 * tok), BF),
            pltpu.VMEM((2 * tok, 2 * tok), F32),
            pltpu.VMEM((3 * tok, chunk), BF),
            pltpu.VMEM((3 * tok, chunk), BF),
            pltpu.VMEM((chunk // per, 4 * tok), F32),
        ],
        compiler_params=pltpu.CompilerParams(vmem_limit_bytes=VMEM),
        name="long",
    )(docs, filt, q, k, v, cot, prod, gm, before, after)


def close_call(docs, mg, x, w, gl, dp, ctx):
    tok, full = x.shape
    depth = ctx // (ACROSS * CORES)
    pair = full // (ACROSS * depth)
    some = gl.shape[0] // (ACROSS * depth)
    taps = gl.shape[1]
    long = gl.reshape(depth, ACROSS, some, taps).transpose(1, 0, 2, 3)
    n3 = dp * CORES - 1
    n = (ACROSS - 1) + (depth - 1) + n3
    piece = 4 * LANES
    space, far = pl.BlockSpec(memory_space=pltpu.VMEM), pl.BlockSpec(memory_space=pl.ANY)
    dma = pltpu.SemaphoreType.DMA
    vm = lambda *s: pltpu.VMEM(s, F32)
    return pl.pallas_call(
        functools.partial(close_kernel, depth, piece),
        out_shape=[
            jax.ShapeDtypeStruct((tok, full), BF),
            jax.ShapeDtypeStruct((3, pair), F32),
            jax.ShapeDtypeStruct((some, taps), F32),
        ],
        in_specs=[space] * 3 + [far] * 2,
        out_specs=[far, space, space],
        scratch_shapes=[
            pltpu.VMEM((tok, full), BF), pltpu.VMEM((tok, full), BF), pltpu.VMEM((tok, full), BF),
            pltpu.VMEM((3, 16, full // 3), BF), pltpu.VMEM((2, full), BF), pltpu.VMEM((2, full), BF),
            pltpu.VMEM((2 * tok, tok), BF), vm(3, 8, LANES), vm(ACROSS, depth, 3, pair),
            vm(ACROSS - 1, depth, 3, pair), vm(ACROSS - 1, depth, some, taps),
            vm(depth - 1, 3, pair), vm(depth - 1, some, taps),
            vm(n3 + 1, 3, pair), vm(n3 + 1, some, taps),
            vm(depth, 3, pair), vm(depth, some, taps),
            dma, dma((full // piece,)), dma((depth,)), dma((depth,)), dma((2,)), dma((2, n)), dma((2, n)),
        ],
        compiler_params=pltpu.CompilerParams(collective_id=1, has_side_effects=True, vmem_limit_bytes=VMEM),
        name="close",
    )(docs, w, long, mg, x)


def local(projected, doc_ids, short_filter, long_filter, cotangent):
    x, cot = projected[0], cotangent[0]
    tok, width = cot.shape
    groups, taps = long_filter.shape
    parts, rows = lax.axis_size("ctx"), lax.axis_size("dp")
    q, k, v, prod, gm, before, after = mix_call(doc_ids, x, short_filter, cot, 512)
    out, mg, gl = long_call(doc_ids, long_filter, q, k, v, cot, prod, gm, before, after, 512)
    gx, gs, gl = close_call(doc_ids, mg, x, short_filter, gl, rows, parts)
    core = lax.axis_index("ctx") % CORES
    gs = lax.dynamic_slice_in_dim(gs, core * (gs.shape[1] // CORES), gs.shape[1] // CORES, 1)
    gl = lax.dynamic_slice_in_dim(gl, core * (gl.shape[0] // CORES), gl.shape[0] // CORES, 0)
    norm = rows * doc_ids.shape[1]
    return out[None], gx[None], gs / math.sqrt(norm), gl / math.sqrt(norm * (width // groups))


def solution(mesh):
    return jax.shard_map(
        local,
        mesh=mesh,
        in_specs=(P("dp", "ctx", None), P("dp", None), P(), P(), P("dp", "ctx", None)),
        out_specs=(P("dp", "ctx", None), P("dp", "ctx", None), P(None, "ctx"), P("ctx", None)),
        check_vma=False,
    )
```

time: 115 us -> 91 us (0.79)
  waiting for transfers between devices: 17.5 us -> 0 us
  starting transfers between devices: 12.6 us -> 0 us
  Pallas kernels: 73.7 us -> 82 us
  local copies, waits for them, and re-layouts: 7.63 us -> 5.39 us
    ppermute x4 -> x0, waiting for transfers between devices: 17.5 us -> none  [passed_along(): lax.ppermute(value, axis, [(s, s + steps) for s in range(first, last)])]
    ppermute x4 -> x0, starting transfers between devices: 12.6 us -> none  [passed_along(): lax.ppermute(value, axis, [(s, s + steps) for s in range(first, last)])]
    pallas_call x3 -> x2, Pallas kernels: 52.3 us -> 60.7 us  [the longest x1 34.4 us: close_call(): pl.pallas_call(functools.partial(close_kernel, depth, piece), out_shape=[...]
    slice x2 -> x0, local copies, waits for them, and re-layouts: 1.94 us -> none  [the longest x1 0.98 us: local(): border = passed_along(x[tok - 2:], 'ctx', 1)]
    reshape x3 -> x1, local copies, waits for them, and re-layouts: 3.4 us -> 1.56 us  [close_call(): long = gl.reshape(depth, ACROSS, some, taps).transpose(1, 0, 2, 3)]
    unnamed x8 -> x1, local copies, waits for them, and re-layouts: 2.3 us -> 3.83 us
  transfers between devices with their start and end apart: 4 -> 0, of which waited for: 4 -> 0; matrix products, arithmetic and copies ran while one was open for 1% -> 0% of each run, Pallas kernels for 0% -> 0%
where the time goes in v2:
time: 91 us; the launch traced here: 90.7 us
  Pallas kernels  82 us (90%)
  local copies, waits for them, and re-layouts  5.39 us (6%)
  other arithmetic  2.62 us (3%)
    pallas_call x1, Pallas kernels, close_call(): pl.pallas_call(functools.partial(close_kernel, depth, piece), out_shape=[...  34.4 us
    pallas_call x1, Pallas kernels, mix_call(): pl.pallas_call(functools.partial(mix_kernel, chunk), out_shape=[shape] *...  26.3 us
    pallas_call x1, Pallas kernels, long_call(): pl.pallas_call(functools.partial(long_kernel, LANES // per), grid=(n,), o...  21.3 us
    unnamed x1, local copies, waits for them, and re-layouts  3.83 us

profile of v2, /device:TPU:1, one launch (start us, length us, event | category | flops | bytes accessed | tf_op | source)
XLA Modules:
  0.0 90.7 jit_solution(16302162482716662855)
XLA Ops:
  0.6 26.3 %mix.1 = (bf16[128,4096]{1,0:T(8,128)(2,1)}, bf16[128,4096]{1,0:T(8,128)(2,1)}, bf16[128,4096]{1,0:T(8,128)(2,1)}, bf16[128,4096]{1,0:T(8,128)(2,1)}, bf16[128,4...) custom-call(s32[1,8192]{1,0:T(1,128)} %doc_ref.5, f32[3,12288]{1,0:T(4,128)} %w_ref.3, ...), custom_call_target="tpu_custom_call" | custom-call | tf_op jit(solution)/shard_map/mix/pallas_call | solution.py:384
  26.9 21.3 %long.1 = (bf16[128,4096]{1,0:T(8,128)(2,1)}, bf16[3,128,4096]{2,1,0:T(8,128)(2,1)}, f32[256,128]{1,0:T(8,128)}) custom-call(s32[1,8192]{1,0:T(1,128)} %doc_ref.5, bf16[256,128]{1,0:T(8,128)(2,1)} %filt_ref.1, bf16[128,4096]{1,0:T(8,128)(2,1)} %get-tuple-element.17.q_ref, bf16[128,4096]{1,0:T(8,128)(2,1)} %get-tuple-element.18.k_ref, ...), custom_call_target="tpu_custom_call" | custom-call | tf_op jit(solution)/shard_map/long/pallas_call | solution.py:408
  48.3 1.6 %copy.11 = f32[8,4,8,128]{3,2,0,1:T(8,128)} copy(f32[8,4,8,128]{3,2,1,0:T(8,128)} %bitcast.14) | data formatting | bytes 262144 | tf_op jit(solution)/shard_map/reshape | solution.py:444
  49.9 34.4 %close.1 = (bf16[128,12288]{1,0:T(8,128)(2,1)}, f32[3,384]{1,0:T(4,128)}, f32[8,128]{1,0:T(8,128)}) custom-call(s32[1,8192]{1,0:T(1,128)} %doc_ref.5, f32[3,12288]{1,0:T(4,128)} %w_ref.3, f32[4,8,8,128]{3,2,1,0:T(8,128)} %bitcast.13, bf16[3,128,4096]{2,1,0:T(8,128)(2,1)} %get-tuple-element.26.mg_hbm, bf16[128,12288]{1,0:T(8,128)(2,1)} %bitcast.9), custom_call_target="tpu_custom_call" | custom-call | tf_op jit(solution)/shard_map/close/pallas_call | solution.py:451
  84.3 1.4 %dynamic-slice_multiply_fusion = f32[3,192]{1,0:T(4,128)} fusion(f32[3,384]{1,0:T(4,128)} %get-tuple-element.28, s32[]{:T(128)S(6)} %select_n.14), kind=kLoop, calls=%fused_computation.1 | loop fusion | flops 576 | bytes 4612 | tf_op jit(solution)/shard_map/div | solution.py:487
  85.6 1.3 %dynamic-slice_multiply_fusion.1 = f32[4,128]{1,0:T(4,128)} fusion(f32[8,128]{1,0:T(8,128)} %get-tuple-element.29, s32[]{:T(128)S(6)} %select_n.15), kind=kLoop, calls=%fused_computation.2 | loop fusion | flops 512 | bytes 4100 | tf_op jit(solution)/shard_map/div | solution.py:487
  86.9 3.8 %copy.13 = bf16[1,128,12288]{2,1,0:T(8,128)(2,1)} copy(bf16[1,128,12288]{2,1,0:T(8,128)(2,1)} %bitcast.12) | data formatting | bytes 6291456

commit v3 on v2

v3 whole, which is shorter than its diff:
```python
import functools
import math

import jax
import jax.numpy as jnp
from jax import lax
from jax.experimental import pallas as pl
from jax.experimental.pallas import tpu as pltpu
from jax.sharding import PartitionSpec as P

BF = jnp.bfloat16
F32 = jnp.float32
MESH = pl.DeviceIdType.MESH
ROWS = 16
LANES = 128
CORES = 2
ACROSS = 4
VMEM = 56 << 20


def near_docs(doc_ref, tok):
    me = lax.axis_index("ctx")
    last = lax.axis_size("ctx") - 1
    at = lambda i: doc_ref[:, pl.ds(pl.multiple_of(i * tok, tok), tok)]
    before = jnp.where(me > 0, at(jnp.maximum(me - 1, 0)), -1)
    after = jnp.where(me < last, at(jnp.minimum(me + 1, last)), -2)
    return jnp.concatenate([before, at(me), after], axis=1).astype(F32)


def doc_column(row):
    return jnp.broadcast_to(row, (row.shape[1], row.shape[1])).T


def shift_matrix(col, row, steps):
    size = col.shape[0]
    place = lax.broadcasted_iota(jnp.int32, (size, size), 1) - lax.broadcasted_iota(jnp.int32, (size, size), 0)
    return jnp.where((place == steps) & (col == row), 1.0, 0.0).astype(BF)


def ring(steps):
    size = lax.axis_size("ctx")
    return lax.axis_index("dp"), (lax.axis_index("ctx") + size + steps) % size


def greet(peers):
    barrier = pltpu.get_barrier_semaphore()
    for peer in peers:
        pl.semaphore_signal(barrier, inc=1, device_id=peer, device_id_type=MESH)
    pl.semaphore_wait(barrier, len(peers))


def sent(src, dst, send, recv, peer):
    return pltpu.make_async_remote_copy(
        src_ref=src, dst_ref=dst, send_sem=send, recv_sem=recv, device_id=peer, device_id_type=MESH
    )


def banded(filt, rows):
    parts = []
    for g in range(filt.shape[0]):
        wide = jnp.broadcast_to(filt[g : g + 1, :], (rows, filt.shape[1]))
        parts.append(pltpu.roll(wide, 0, 1, stride=1, stride_axis=0).astype(BF))
    return parts


def diagonal_sums(part, width):
    half = part.shape[0] // 2
    while half >= 8:
        part = part[:half] + pltpu.roll(part[half:], width - half, 1)
        half //= 2
    while half >= 1:
        part = part + pltpu.roll(pltpu.roll(part, 8 - half, 0), width - half, 1)
        half //= 2
    return part[0:1]


def whole_kernel(groups, chunk, depth, scales, doc_ref, w_ref, filt_ref, x_hbm, cot_hbm, out_hbm, gx_hbm, s_out, l_out,
                 xs, cs, qs, ks, vs, pwin, gwin, mg, ys, outs, tail, mine, border, heads, ahead,
                 back_shift, fore_shift, back_edge, fore_edge, keeps, keeps32, wide_filt, ssum, lsum,
                 s1, l1, s2, l2, s3, l3, bs, bl,
                 tail_sem, in_sem, out_sem, y_sem, edge_sem, blk_send, blk_recv, row_send, row_recv, send, recv):
    rows = ROWS
    tok, width = cs.shape
    full = 3 * width
    steps = tok // rows
    count = width // chunk
    blocks = chunk // LANES
    wide = 2 * LANES
    dp, ctx = lax.axis_index("dp"), lax.axis_index("ctx")
    z, x, c = ctx // (ACROSS * CORES), (ctx // CORES) % ACROSS, ctx % CORES
    place = lambda zz, xx, cc: (zz * ACROSS + xx) * CORES + cc
    dps = lax.axis_size("dp")
    across = [(dp, place(z, (x + d) % ACROSS, c)) for d in range(1, ACROSS)]
    along = [(dp, place((z + d) % depth, x, c)) for d in range(1, depth)]
    final = [((dp + d // CORES) % dps, place(z, x, (c + d) % CORES)) for d in range(1, dps * CORES)]
    n1, n2, n3 = len(across), len(along), len(final)
    right, left = ring(1), ring(-1)

    def at(i, size=chunk, offset=0):
        return pl.ds(pl.multiple_of(offset + i * size, LANES), size)

    def loads(i):
        for p in range(3):
            here = at(i, offset=p * width)
            yield pltpu.make_async_copy(x_hbm.at[:, here], xs.at[:, here], in_sem.at[p, i])
        yield pltpu.make_async_copy(cot_hbm.at[:, at(i)], cs.at[:, at(i)], in_sem.at[3, i])

    def block_sends(i):
        own = pl.ds(tok, tok), pl.ds(0, tok)
        yield sent(pwin.at[own[0], at(i)], pwin.at[own[1], at(i)], blk_send.at[0, i], blk_recv.at[0, i], right)
        yield sent(gwin.at[own[1], at(i)], gwin.at[own[0], at(i)], blk_send.at[1, i], blk_recv.at[1, i], left)

    def row_sends(i):
        for p in range(3):
            here = at(i, offset=p * width)
            yield sent(heads.at[:, here], ahead.at[:, here], row_send.at[p, i], row_recv.at[p, i], left)

    def out_save(i):
        return pltpu.make_async_copy(outs.at[:, at(i)], out_hbm.at[:, at(i)], out_sem.at[i])

    slab = full // depth

    def y_save(i):
        return pltpu.make_async_copy(ys.at[:, at(i, slab)], gx_hbm.at[:, at(i, slab)], y_sem.at[i])

    def first_exchange(src, dst, k):
        return [sent(src.at[(x + d) % ACROSS], dst.at[d - 1], send.at[k, d - 1], recv.at[k, d - 1], across[d - 1])
                for d in range(1, ACROSS)]

    def second_exchange(src, dst, k):
        return [sent(src.at[(z + d) % depth], dst.at[d - 1], send.at[k, n1 + d - 1], recv.at[k, n1 + d - 1], along[d - 1])
                for d in range(1, depth)]

    def third_exchange(buf, k):
        return [sent(buf.at[n3], buf.at[d], send.at[k, n1 + n2 + d], recv.at[k, n1 + n2 + d], final[d])
                for d in range(n3)]

    def begin(copies):
        for copy in copies:
            copy.start()

    def arrive(copies):
        for copy in copies:
            copy.wait_recv()

    def total(start, arrived, n):
        for i in range(n):
            start = start + arrived[i]
        return start

    first = pltpu.make_async_copy(x_hbm.at[tok - 16 :, :], tail, tail_sem)
    first.start()
    for i in range(count):
        begin(loads(i))
    peers = [right, left] + across + along + final
    barrier = pltpu.get_barrier_semaphore()
    for peer in peers:
        pl.semaphore_signal(barrier, inc=1, device_id=peer, device_id_type=MESH)
    first.wait()
    mine[...] = tail[14:16, :]
    pl.semaphore_wait(barrier, len(peers))
    edge_copy = sent(mine, border, edge_sem.at[0], edge_sem.at[1], right)
    edge_copy.start()

    docs = near_docs(doc_ref, tok)
    own = docs[:, tok : 2 * tok]
    col = doc_column(own)
    for shifts, sign in ((back_shift, -1), (fore_shift, 1)):
        shifts[0:tok, :] = shift_matrix(col, own, sign)
        shifts[tok:, :] = shift_matrix(col, own, 2 * sign)
    row = lax.broadcasted_iota(jnp.int32, (8, LANES), 0)
    spread_doc = lambda d: jnp.broadcast_to(docs[:, d : d + 1], (8, LANES))
    top, end = col[:8, :], col[tok - 8 :, :]
    old, new = [spread_doc(tok - 1), spread_doc(tok - 2)], [spread_doc(2 * tok), spread_doc(2 * tok + 1)]
    back_edge[0] = jnp.where((row == 0) & (top == old[0]), 1.0, 0.0)
    back_edge[1] = jnp.where((row == 0) & (top == old[1]), 1.0, 0.0)
    back_edge[2] = jnp.where((row == 1) & (top == old[0]), 1.0, 0.0)
    fore_edge[0] = jnp.where((row == 7) & (end == new[0]), 1.0, 0.0)
    fore_edge[1] = jnp.where((row == 6) & (end == new[0]), 1.0, 0.0)
    fore_edge[2] = jnp.where((row == 7) & (end == new[1]), 1.0, 0.0)
    edge_copy.wait()

    def mixed(i, j, part):
        here = pl.ds(pl.multiple_of(part * width + i * chunk + j * wide, LANES), wide)
        edges = [jnp.concatenate([back_edge[n]] * 2, axis=1) for n in range(3)]
        value = xs[:, here]
        moved = jnp.dot(back_shift[...], value, preferred_element_type=F32)
        side = border[:, here].astype(F32)
        w = w_ref[:, here]
        mix = w[0:1] * value.astype(F32) + w[1:2] * moved[:tok] + w[2:3] * moved[tok:]
        fix = w[1:2] * (edges[0] * side[1:2]) + w[2:3] * (edges[1] * side[0:1] + edges[2] * side[1:2])
        return jnp.concatenate([mix[:8] + fix, mix[8:]], axis=0).astype(BF)

    def mix_step(i, carry):
        for copy in loads(i):
            copy.wait()
        for j in range(chunk // wide):
            here = pl.ds(pl.multiple_of(i * chunk + j * wide, LANES), wide)
            q, k, v = mixed(i, j, 0), mixed(i, j, 1), mixed(i, j, 2)
            qs[:, here], ks[:, here], vs[:, here] = q, k, v
            gwin[0:tok, here] = (cs[:, here].astype(F32) * q.astype(F32)).astype(BF)
            pwin[tok : 2 * tok, here] = (k.astype(F32) * v.astype(F32)).astype(BF)
        begin(block_sends(i))
        return carry

    lax.fori_loop(0, count, mix_step, 0)

    both = jnp.concatenate([col, col], axis=1)
    long_row = jnp.concatenate([jnp.broadcast_to(docs, (8, 3 * tok)), jnp.full((8, tok), -3.0, F32)], axis=1)
    for a in range(steps):
        block_docs = both[a * rows : (a + 1) * rows]
        for b, start in ((a, a * rows), (steps + a, tok + a * rows)):
            window = pltpu.roll(long_row, (4 * tok - start) % (4 * tok), 1)[0:1, : 2 * tok]
            keep = jnp.where(block_docs == window, 1.0, 0.0)
            keeps32[b * rows : (b + 1) * rows, :] = keep
            keeps[b * rows : (b + 1) * rows, :] = keep.astype(BF)
    pwin[2 * tok :, :] = jnp.zeros((tok, width), BF)
    gwin[2 * tok :, :] = jnp.zeros((tok, width), BF)
    filt = filt_ref[...]
    turn = lax.broadcasted_iota(jnp.int32, (tok, tok), 0) + lax.broadcasted_iota(jnp.int32, (tok, tok), 1)
    wide_filt[:, 0:tok] = jnp.dot(filt, jnp.where(turn == tok, 1.0, 0.0).astype(BF), preferred_element_type=F32)
    filt = filt.astype(F32)
    lane = lax.broadcasted_iota(jnp.int32, filt.shape, 1)
    wide_filt[:, tok : 2 * tok] = jnp.where(lane == 0, filt, 0.0)
    wide_filt[:, 2 * tok : 3 * tok] = filt
    wide_filt[:, 3 * tok :] = jnp.zeros(filt.shape, F32)

    lane_group = lax.broadcasted_iota(jnp.int32, (rows, LANES), 1) // (LANES // groups)

    def pick(value):
        chosen = value[:rows]
        for g in range(1, groups):
            chosen = jnp.where(lane_group == g, value[g * rows : (g + 1) * rows], chosen)
        return chosen

    per_z = count * blocks // depth
    per_x = per_z // ACROSS

    def long_step(i, carry):
        arrive(block_sends(i))
        for j in range(blocks):
            part = [pl.ds(pl.multiple_of(p * width + i * chunk + j * LANES, LANES), LANES) for p in range(3)]
            here = part[0]
            b = i * blocks + j
            own = pl.ds(pl.multiple_of(b * groups, groups), groups)
            lead = banded(wide_filt[own, : 2 * tok], rows)
            back = banded(wide_filt[own, 2 * tok :], rows)
            diag = None
            for a in range(steps):
                now = slice(a * rows, (a + 1) * rows)
                next_rows = slice((steps + a) * rows, (steps + a + 1) * rows)
                span = slice(a * rows, a * rows + 2 * tok)
                keep = keeps[now, :]
                mix = jnp.dot(jnp.concatenate([t * keep for t in lead], axis=0), pwin[span, here], preferred_element_type=F32)
                mix = pick(mix).astype(BF).astype(F32)
                outs[now, here] = (qs[now, here].astype(F32) * mix).astype(BF)
                g_q = (cs[now, here].astype(F32) * mix).astype(BF)
                keep = keeps[next_rows, :]
                grad = jnp.dot(jnp.concatenate([t * keep for t in back], axis=0), gwin[span, here], preferred_element_type=F32)
                grad = pick(grad).astype(BF).astype(F32)
                g_k = (grad * vs[now, here].astype(F32)).astype(BF)
                g_v = (grad * ks[now, here].astype(F32)).astype(BF)
                for p, value in enumerate((g_q, g_k, g_v)):
                    mg[now, part[p]] = value
                    if a == 0:
                        heads[:, part[p]] = value[0:2]
                mine_prod = pwin[tok + a * rows : tok + (a + 1) * rows, here]
                zero = jnp.zeros_like(mine_prod)
                spread = jnp.concatenate([jnp.where(lane_group == g, mine_prod, zero) for g in range(groups)], axis=0)
                pairs = lax.dot_general(spread, gwin[span, here], (((1,), (1,)), ((), ())), preferred_element_type=F32)
                keep = keeps32[next_rows, :]
                pairs = [pairs[g * rows : (g + 1) * rows] * keep for g in range(groups)]
                diag = pairs if diag is None else [s + t for s, t in zip(diag, pairs)]
            sums = jnp.concatenate([diagonal_sums(d, 2 * tok)[:, :tok] for d in diag], axis=0)
            lsum[(b % per_z) // per_x, b // per_z, pl.ds(pl.multiple_of(b % per_x * groups, groups), groups), :] = sums
        begin(row_sends(i))
        out_save(i).start()
        return carry

    lax.fori_loop(0, count, long_step, 0)
    long_one = first_exchange(lsum, l1, 1)
    begin(long_one)
    for i in range(count):
        arrive(row_sends(i))

    pair = slab // ACROSS

    def close_step(i, carry):
        edges = [jnp.concatenate([fore_edge[n]] * (pair // LANES), axis=1) for n in range(3)]
        for j in range(ACROSS):
            here = pl.ds(pl.multiple_of(i * slab + j * pair, LANES), pair)
            g = mg[:, here]
            moved = jnp.dot(fore_shift[...], g, preferred_element_type=F32)
            side = ahead[:, here].astype(F32)
            one, two = moved[:tok], moved[tok:]
            one = jnp.concatenate([one[: tok - 8], one[tok - 8 :] + edges[0] * side[0:1]], axis=0)
            two = jnp.concatenate(
                [two[: tok - 8], two[tok - 8 :] + edges[1] * side[0:1] + edges[2] * side[1:2]], axis=0
            )
            g = g.astype(F32)
            w = w_ref[:, here]
            ys[:, here] = (w[0:1] * g + w[1:2] * one + w[2:3] * two).astype(BF)
            source = xs[:, here].astype(F32)
            ssum[j, i] = jnp.concatenate(
                [jnp.sum(moved_grad * source, axis=0, keepdims=True) for moved_grad in (g, one, two)], axis=0
            )
        y_save(i).start()
        return carry

    half = depth // 2
    lax.fori_loop(0, half, close_step, 0)
    arrive(long_one)
    bl[...] = total(lsum[x], l1, n1)
    long_two = second_exchange(bl, l2, 1)
    begin(long_two)
    lax.fori_loop(half, depth, close_step, 0)
    short_one = first_exchange(ssum, s1, 0)
    begin(short_one)
    arrive(long_two)
    l3[n3] = total(bl[z], l2, n2)
    long_three = third_exchange(l3, 1)
    begin(long_three)
    arrive(short_one)
    bs[...] = total(ssum[x], s1, n1)
    short_two = second_exchange(bs, s2, 0)
    begin(short_two)
    arrive(long_three)
    sums = total(l3[n3], l3, n3) * scales[1]
    l_out[...] = jnp.where(c == 0, sums[: sums.shape[0] // CORES], sums[sums.shape[0] // CORES :])
    arrive(short_two)
    s3[n3] = total(bs[z], s2, n2)
    short_three = third_exchange(s3, 0)
    begin(short_three)
    for i in range(depth):
        y_save(i).wait()
    for i in range(count):
        out_save(i).wait()
        for copy in list(block_sends(i)) + list(row_sends(i)):
            copy.wait_send()
    arrive(short_three)
    sums = total(s3[n3], s3, n3) * scales[0]
    s_out[...] = jnp.where(c == 0, sums[:, : pair // CORES], sums[:, pair // CORES :])
    for copy in long_one + long_two + long_three + short_one + short_two + short_three:
        copy.wait_send()


def local(projected, doc_ids, short_filter, long_filter, cotangent):
    x, cot = projected[0], cotangent[0]
    tok, width = cot.shape
    full = 3 * width
    groups, taps = long_filter.shape
    dps, ctx = lax.axis_size("dp"), lax.axis_size("ctx")
    depth = ctx // (ACROSS * CORES)
    pair = full // (ACROSS * depth)
    some = groups // (ACROSS * depth)
    chunk = 4 * LANES
    n = width // chunk
    n3 = dps * CORES - 1
    links = (ACROSS - 1) + (depth - 1) + n3
    norm = dps * doc_ids.shape[1]
    scales = (1.0 / math.sqrt(norm), 1.0 / math.sqrt(norm * (width // groups)))
    space, far = pl.BlockSpec(memory_space=pltpu.VMEM), pl.BlockSpec(memory_space=pl.ANY)
    dma = pltpu.SemaphoreType.DMA
    half = lambda *s: pltpu.VMEM(s, BF)
    word = lambda *s: pltpu.VMEM(s, F32)
    out, gx, gs, gl = pl.pallas_call(
        functools.partial(whole_kernel, LANES // (width // groups), chunk, depth, scales),
        out_shape=[
            jax.ShapeDtypeStruct((tok, width), BF),
            jax.ShapeDtypeStruct((tok, full), BF),
            jax.ShapeDtypeStruct((3, pair // CORES), F32),
            jax.ShapeDtypeStruct((some // CORES, taps), F32),
        ],
        in_specs=[space] * 3 + [far] * 2,
        out_specs=[far, far, space, space],
        scratch_shapes=[
            half(tok, full), half(tok, width), half(tok, width), half(tok, width), half(tok, width),
            half(3 * tok, width), half(3 * tok, width), half(tok, full), half(tok, full), half(tok, width),
            half(16, full), half(2, full), half(2, full), half(2, full), half(2, full),
            half(2 * tok, tok), half(2 * tok, tok), word(3, 8, LANES), word(3, 8, LANES),
            half(2 * tok, 2 * tok), word(2 * tok, 2 * tok), word(groups, 4 * tok),
            word(ACROSS, depth, 3, pair), word(ACROSS, depth, some, taps),
            word(ACROSS - 1, depth, 3, pair), word(ACROSS - 1, depth, some, taps),
            word(depth - 1, 3, pair), word(depth - 1, some, taps),
            word(n3 + 1, 3, pair), word(n3 + 1, some, taps),
            word(depth, 3, pair), word(depth, some, taps),
            dma, dma((4, n)), dma((n,)), dma((depth,)), dma((2,)), dma((2, n)), dma((2, n)),
            dma((3, n)), dma((3, n)), dma((2, links)), dma((2, links)),
        ],
        compiler_params=pltpu.CompilerParams(collective_id=0, has_side_effects=True, vmem_limit_bytes=VMEM),
        name="whole",
    )(doc_ids, short_filter, long_filter, x, cot)
    return out[None], gx[None], gs, gl


def solution(mesh):
    return jax.shard_map(
        local,
        mesh=mesh,
        in_specs=(P("dp", "ctx", None), P("dp", None), P(), P(), P("dp", "ctx", None)),
        out_specs=(P("dp", "ctx", None), P("dp", "ctx", None), P(None, "ctx"), P("ctx", None)),
        check_vma=False,
    )
```

time: 91 us -> 68 us (0.75)
  Pallas kernels: 82 us -> 59.9 us
  other arithmetic: 2.62 us -> 0 us
  local copies, waits for them, and re-layouts: 5.39 us -> 7.3 us
    pallas_call x3 -> x1, Pallas kernels: 82 us -> 59.9 us  [local(): pl.pallas_call(functools.partial(whole_kernel, LANES // (width // groups)...]
    unnamed x1 -> x8, local copies, waits for them, and re-layouts: 3.83 us -> 7.3 us
    div x2 -> x0, other arithmetic: 2.62 us -> none  [the longest x1 1.35 us: local(): gs / math.sqrt(norm)]
    reshape x1 -> x0, local copies, waits for them, and re-layouts: 1.56 us -> none  [close_call(): long = gl.reshape(depth, ACROSS, some, taps).transpose(1, 0, 2, 3)]
where the time goes in v3:
time: 68 us; the launch traced here: 67.8 us
  Pallas kernels  59.9 us (88%)
  local copies, waits for them, and re-layouts  7.3 us (11%)
    pallas_call x1, Pallas kernels, local(): pl.pallas_call(functools.partial(whole_kernel, LANES // (width // groups)...  59.9 us
    unnamed x8, local copies, waits for them, and re-layouts  7.3 us

profile of v3, /device:TPU:1, one launch (start us, length us, event | category | flops | bytes accessed | tf_op | source)
XLA Modules:
  0.0 67.8 jit_solution(2054302435300175555)
XLA Ops:
  0.6 59.9 %whole.1 = (bf16[128,4096]{1,0:T(8,128)(2,1)}, bf16[128,12288]{1,0:T(8,128)(2,1)}, f32[3,192]{1,0:T(4,128)}, f32[4,128]{1,0:T(4,128)}) custom-call(s32[1,8192]{1,0:T(1,128)} %doc_ref.1, f32[3,12288]{1,0:T(4,128)} %w_ref.1, bf16[256,128]{1,0:T(8,128)(2,1)} %filt_ref.1, bf16[128,12288]{1,0:T(8,128)(2,1)} %bitcast.4, bf16[128,4096]{1,0:T(8,128)(2,1)} %bitcast.6), custom_call_target="tpu_custom_call" | custom-call | tf_op jit(solution)/shard_map/whole/pallas_call | solution.py:366
  60.5 2.3 %copy.13 = bf16[1,128,4096]{2,1,0:T(8,128)(2,1)} copy(bf16[1,128,4096]{2,1,0:T(8,128)(2,1)} %bitcast.7) | data formatting | bytes 2097152
  62.8 0.0 copy-start
  62.8 0.0 copy-start.1
  62.8 3.8 %copy.14 = bf16[1,128,12288]{2,1,0:T(8,128)(2,1)} copy(bf16[1,128,12288]{2,1,0:T(8,128)(2,1)} %bitcast.5) | data formatting | bytes 6291456
  66.7 0.0 copy-done
  66.7 0.6 copy.15
  67.2 0.0 copy-done.1
  67.3 0.6 copy.16
Async XLA Ops:
  62.8 3.8 %copy-start = (f32[3,192]{1,0:T(4,128)S(1)}, f32[3,192]{1,0:T(4,128)}, u32[]{:S(2)}) copy-start(f32[3,192]{1,0:T(4,128)} %get-tuple-element.18) | copy-start | bytes 6916
  62.8 4.4 %copy-start.1 = (f32[4,128]{1,0:T(4,128)S(1)}, f32[4,128]{1,0:T(4,128)}, u32[]{:S(2)}) copy-start(f32[4,128]{1,0:T(4,128)} %get-tuple-element.19) | copy-start | bytes 6148

commit v4 on v3

--- a/solution.py
+++ b/solution.py
@@ -15,6 +15,7 @@
 LANES = 128
 CORES = 2
 ACROSS = 4
+CUTS = 2
 VMEM = 56 << 20
 
 
@@ -40,13 +41,6 @@
 def ring(steps):
     size = lax.axis_size("ctx")
     return lax.axis_index("dp"), (lax.axis_index("ctx") + size + steps) % size
-
-
-def greet(peers):
-    barrier = pltpu.get_barrier_semaphore()
-    for peer in peers:
-        pl.semaphore_signal(barrier, inc=1, device_id=peer, device_id_type=MESH)
-    pl.semaphore_wait(barrier, len(peers))
 
 
 def sent(src, dst, send, recv, peer):
@@ -78,7 +72,7 @@
                  xs, cs, qs, ks, vs, pwin, gwin, mg, ys, outs, tail, mine, border, heads, ahead,
                  back_shift, fore_shift, back_edge, fore_edge, keeps, keeps32, wide_filt, ssum, lsum,
                  s1, l1, s2, l2, s3, l3, bs, bl,
-                 tail_sem, in_sem, out_sem, y_sem, edge_sem, blk_send, blk_recv, row_send, row_recv, send, recv):
+                 tail_sem, in_sem, out_sem, y_sem, edge_sem, blk_send, blk_recv, row_send, row_recv, x_send, x_recv, z_sem, send, recv):
     rows = ROWS
     tok, width = cs.shape
     full = 3 * width
@@ -121,14 +115,27 @@
     slab = full // depth
 
     def y_save(i):
-        return pltpu.make_async_copy(ys.at[:, at(i, slab)], gx_hbm.at[:, at(i, slab)], y_sem.at[i])
-
-    def first_exchange(src, dst, k):
-        return [sent(src.at[(x + d) % ACROSS], dst.at[d - 1], send.at[k, d - 1], recv.at[k, d - 1], across[d - 1])
+        here = at((z + 1 + i) % depth, slab)
+        return pltpu.make_async_copy(ys.at[:, here], gx_hbm.at[:, here], y_sem.at[i])
+
+    def slab_of(i):
+        return (z + 1 + i) % depth
+
+    def x_sends(i):
+        to = slab_of(i)
+        return [sent(ssum.at[(x + d) % ACROSS, to], s1.at[d - 1, to], x_send.at[d - 1, i], x_recv.at[d - 1, i], across[d - 1])
                 for d in range(1, ACROSS)]
 
-    def second_exchange(src, dst, k):
-        return [sent(src.at[(z + d) % depth], dst.at[d - 1], send.at[k, n1 + d - 1], recv.at[k, n1 + d - 1], along[d - 1])
+    def z_send(i):
+        to = slab_of(i)
+        return sent(bs.at[to], s2.at[i], z_sem.at[0, i], z_sem.at[1, i], (dp, place(to, x, c)))
+
+    def long_across():
+        return [sent(lsum.at[(x + d) % ACROSS], l1.at[d - 1], send.at[1, d - 1], recv.at[1, d - 1], across[d - 1])
+                for d in range(1, ACROSS)]
+
+    def long_along():
+        return [sent(bl.at[(z + d) % depth], l2.at[d - 1], send.at[1, n1 + d - 1], recv.at[1, n1 + d - 1], along[d - 1])
                 for d in range(1, depth)]
 
     def third_exchange(buf, k):
@@ -178,33 +185,6 @@
     fore_edge[0] = jnp.where((row == 7) & (end == new[0]), 1.0, 0.0)
     fore_edge[1] = jnp.where((row == 6) & (end == new[0]), 1.0, 0.0)
     fore_edge[2] = jnp.where((row == 7) & (end == new[1]), 1.0, 0.0)
-    edge_copy.wait()
-
-    def mixed(i, j, part):
-        here = pl.ds(pl.multiple_of(part * width + i * chunk + j * wide, LANES), wide)
-        edges = [jnp.concatenate([back_edge[n]] * 2, axis=1) for n in range(3)]
-        value = xs[:, here]
-        moved = jnp.dot(back_shift[...], value, preferred_element_type=F32)
-        side = border[:, here].astype(F32)
-        w = w_ref[:, here]
-        mix = w[0:1] * value.astype(F32) + w[1:2] * moved[:tok] + w[2:3] * moved[tok:]
-        fix = w[1:2] * (edges[0] * side[1:2]) + w[2:3] * (edges[1] * side[0:1] + edges[2] * side[1:2])
-        return jnp.concatenate([mix[:8] + fix, mix[8:]], axis=0).astype(BF)
-
-    def mix_step(i, carry):
-        for copy in loads(i):
-            copy.wait()
-        for j in range(chunk // wide):
-            here = pl.ds(pl.multiple_of(i * chunk + j * wide, LANES), wide)
-            q, k, v = mixed(i, j, 0), mixed(i, j, 1), mixed(i, j, 2)
-            qs[:, here], ks[:, here], vs[:, here] = q, k, v
-            gwin[0:tok, here] = (cs[:, here].astype(F32) * q.astype(F32)).astype(BF)
-            pwin[tok : 2 * tok, here] = (k.astype(F32) * v.astype(F32)).astype(BF)
-        begin(block_sends(i))
-        return carry
-
-    lax.fori_loop(0, count, mix_step, 0)
-
     both = jnp.concatenate([col, col], axis=1)
     long_row = jnp.concatenate([jnp.broadcast_to(docs, (8, 3 * tok)), jnp.full((8, tok), -3.0, F32)], axis=1)
     for a in range(steps):
@@ -224,6 +204,32 @@
     wide_filt[:, tok : 2 * tok] = jnp.where(lane == 0, filt, 0.0)
     wide_filt[:, 2 * tok : 3 * tok] = filt
     wide_filt[:, 3 * tok :] = jnp.zeros(filt.shape, F32)
+    edge_copy.wait()
+
+    def mixed(i, j, part):
+        here = pl.ds(pl.multiple_of(part * width + i * chunk + j * wide, LANES), wide)
+        edges = [jnp.concatenate([back_edge[n]] * 2, axis=1) for n in range(3)]
+        value = xs[:, here]
+        moved = jnp.dot(back_shift[...], value, preferred_element_type=F32)
+        side = border[:, here].astype(F32)
+        w = w_ref[:, here]
+        mix = w[0:1] * value.astype(F32) + w[1:2] * moved[:tok] + w[2:3] * moved[tok:]
+        fix = w[1:2] * (edges[0] * side[1:2]) + w[2:3] * (edges[1] * side[0:1] + edges[2] * side[1:2])
+        return jnp.concatenate([mix[:8] + fix, mix[8:]], axis=0).astype(BF)
+
+    def mix_step(i, carry):
+        for copy in loads(i):
+            copy.wait()
+        for j in range(chunk // wide):
+            here = pl.ds(pl.multiple_of(i * chunk + j * wide, LANES), wide)
+            q, k, v = mixed(i, j, 0), mixed(i, j, 1), mixed(i, j, 2)
+            qs[:, here], ks[:, here], vs[:, here] = q, k, v
+            gwin[0:tok, here] = (cs[:, here].astype(F32) * q.astype(F32)).astype(BF)
+            pwin[tok : 2 * tok, here] = (k.astype(F32) * v.astype(F32)).astype(BF)
+        begin(block_sends(i))
+        return carry
+
+    lax.fori_loop(0, count, mix_step, 0)
 
     lane_group = lax.broadcasted_iota(jnp.int32, (rows, LANES), 1) // (LANES // groups)
 
@@ -278,17 +284,18 @@
         return carry
 
     lax.fori_loop(0, count, long_step, 0)
-    long_one = first_exchange(lsum, l1, 1)
+    long_one = long_across()
     begin(long_one)
     for i in range(count):
         arrive(row_sends(i))
 
     pair = slab // ACROSS
 
-    def close_step(i, carry):
+    def close_slab(i):
+        to = slab_of(i)
         edges = [jnp.concatenate([fore_edge[n]] * (pair // LANES), axis=1) for n in range(3)]
         for j in range(ACROSS):
-            here = pl.ds(pl.multiple_of(i * slab + j * pair, LANES), pair)
+            here = pl.ds(pl.multiple_of(to * slab + j * pair, LANES), pair)
             g = mg[:, here]
             moved = jnp.dot(fore_shift[...], g, preferred_element_type=F32)
             side = ahead[:, here].astype(F32)
@@ -301,47 +308,83 @@
             w = w_ref[:, here]
             ys[:, here] = (w[0:1] * g + w[1:2] * one + w[2:3] * two).astype(BF)
             source = xs[:, here].astype(F32)
-            ssum[j, i] = jnp.concatenate(
+            ssum[j, to] = jnp.concatenate(
                 [jnp.sum(moved_grad * source, axis=0, keepdims=True) for moved_grad in (g, one, two)], axis=0
             )
+        begin(x_sends(i))
         y_save(i).start()
+
+    def pass_on(i):
+        arrive(x_sends(i))
+        to = slab_of(i)
+        bs[to] = total(ssum[x, to], [s1[d, to] for d in range(n1)], n1)
+
+    def close_step(i, carry):
+        close_slab(i)
         return carry
 
     half = depth // 2
     lax.fori_loop(0, half, close_step, 0)
     arrive(long_one)
     bl[...] = total(lsum[x], l1, n1)
-    long_two = second_exchange(bl, l2, 1)
+    long_two = long_along()
     begin(long_two)
     lax.fori_loop(half, depth, close_step, 0)
-    short_one = first_exchange(ssum, s1, 0)
-    begin(short_one)
+    for i in range(n2):
+        pass_on(i)
+        z_send(i).start()
     arrive(long_two)
     l3[n3] = total(bl[z], l2, n2)
     long_three = third_exchange(l3, 1)
     begin(long_three)
-    arrive(short_one)
-    bs[...] = total(ssum[x], s1, n1)
-    short_two = second_exchange(bs, s2, 0)
-    begin(short_two)
+    pass_on(depth - 1)
+    for i in range(n2):
+        z_send(i).wait_recv()
+    s3[n3] = total(bs[z], s2, n2)
+    short_three = third_exchange(s3, 0)
+    begin(short_three)
     arrive(long_three)
     sums = total(l3[n3], l3, n3) * scales[1]
     l_out[...] = jnp.where(c == 0, sums[: sums.shape[0] // CORES], sums[sums.shape[0] // CORES :])
-    arrive(short_two)
-    s3[n3] = total(bs[z], s2, n2)
-    short_three = third_exchange(s3, 0)
-    begin(short_three)
     for i in range(depth):
         y_save(i).wait()
+        for copy in x_sends(i):
+            copy.wait_send()
+    for i in range(n2):
+        z_send(i).wait_send()
     for i in range(count):
         out_save(i).wait()
         for copy in list(block_sends(i)) + list(row_sends(i)):
             copy.wait_send()
+    for copy in long_one + long_two + long_three:
+        copy.wait_send()
     arrive(short_three)
     sums = total(s3[n3], s3, n3) * scales[0]
     s_out[...] = jnp.where(c == 0, sums[:, : pair // CORES], sums[:, pair // CORES :])
-    for copy in long_one + long_two + long_three + short_one + short_two + short_three:
+    for copy in short_three:
         copy.wait_send()
+
+
+def copy_kernel(*refs):
+    count = len(refs) // 2
+    for src, dst in zip(refs[:count], refs[count:]):
+        dst[...] = src[...]
+
+
+def copied(large, small, cuts):
+    def spec(a):
+        return pl.BlockSpec((a.shape[0] // cuts, a.shape[1]), lambda i: (i, 0))
+
+    specs = [spec(a) for a in large] + [pl.BlockSpec(a.shape, lambda i: (0, 0)) for a in small]
+    return pl.pallas_call(
+        copy_kernel,
+        grid=(cuts,),
+        out_shape=[jax.ShapeDtypeStruct(a.shape, a.dtype) for a in large + small],
+        in_specs=specs,
+        out_specs=specs,
+        compiler_params=pltpu.CompilerParams(vmem_limit_bytes=VMEM),
+        name="place",
+    )(*large, *small)
 
 
 def local(projected, doc_ids, short_filter, long_filter, cotangent):
@@ -385,11 +428,13 @@
             word(n3 + 1, 3, pair), word(n3 + 1, some, taps),
             word(depth, 3, pair), word(depth, some, taps),
             dma, dma((4, n)), dma((n,)), dma((depth,)), dma((2,)), dma((2, n)), dma((2, n)),
-            dma((3, n)), dma((3, n)), dma((2, links)), dma((2, links)),
+            dma((3, n)), dma((3, n)), dma((ACROSS - 1, depth)), dma((ACROSS - 1, depth)), dma((2, depth)),
+            dma((2, links)), dma((2, links)),
         ],
         compiler_params=pltpu.CompilerParams(collective_id=0, has_side_effects=True, vmem_limit_bytes=VMEM),
         name="whole",
     )(doc_ids, short_filter, long_filter, x, cot)
+    out, gx, gs, gl = copied([out, gx], [gs, gl], CUTS)
     return out[None], gx[None], gs, gl
 
 

time: 68 us -> 61.9 us (0.910)
  local copies, waits for them, and re-layouts: 7.3 us -> 0 us
  Pallas kernels: 59.9 us -> 61.1 us
    unnamed x8 -> x0, local copies, waits for them, and re-layouts: 7.3 us -> none
    pallas_call x0 -> x1, Pallas kernels: none -> 3.75 us  [copied(): pl.pallas_call(copy_kernel, grid=(cuts,), out_shape=[jax.ShapeDtypeStruct...]
    pallas_call x1, Pallas kernels: 59.9 us -> 57.4 us  [local(): pl.pallas_call(functools.partial(whole_kernel, LANES // (width // groups)...]
where the time goes in v4:
time: 61.9 us; the launch traced here: 61.8 us
  Pallas kernels  61.1 us (99%)
  between operations  0.64 us (1%)
    pallas_call x1, Pallas kernels, local(): pl.pallas_call(functools.partial(whole_kernel, LANES // (width // groups)...  57.4 us
    pallas_call x1, Pallas kernels, copied(): pl.pallas_call(copy_kernel, grid=(cuts,), out_shape=[jax.ShapeDtypeStruct...  3.75 us

profile of v4, /device:TPU:1, one launch (start us, length us, event | category | flops | bytes accessed | tf_op | source)
XLA Modules:
  0.0 61.8 jit_solution(15817202244504769583)
XLA Ops:
  0.6 57.4 %whole.1 = (bf16[128,4096]{1,0:T(8,128)(2,1)}, bf16[128,12288]{1,0:T(8,128)(2,1)}, f32[3,192]{1,0:T(4,128)}, f32[4,128]{1,0:T(4,128)}) custom-call(s32[1,8192]{1,0:T(1,128)} %doc_ref.1, f32[3,12288]{1,0:T(4,128)} %w_ref.1, bf16[256,128]{1,0:T(8,128)(2,1)} %filt_ref.1, bf16[128,12288]{1,0:T(8,128)(2,1)} %bitcast.4, bf16[128,4096]{1,0:T(8,128)(2,1)} %bitcast.5), custom_call_target="tpu_custom_call" | custom-call | tf_op jit(solution)/shard_map/whole/pallas_call | solution.py:409
  58.0 3.7 %place.1 = (bf16[128,4096]{1,0:T(8,128)(2,1)}, bf16[128,12288]{1,0:T(8,128)(2,1)}, f32[3,192]{1,0:T(4,128)}, f32[4,128]{1,0:T(4,128)}) custom-call(bf16[128,4096]{1,0:T(8,128)(2,1)} %get-tuple-element.12.refs_0_, bf16[128,12288]{1,0:T(8,128)(2,1)} %get-tuple-element.13.refs_1_, f32[3,192]{1,0:T(4,128)} %get-tuple-element.14.refs_2_, ...), custom_call_target="tpu_custom_call" | custom-call | tf_op jit(solution)/shard_map/place/pallas_call | solution.py:379

commit v5 on v4

--- a/solution.py
+++ b/solution.py
@@ -16,7 +16,7 @@
 CORES = 2
 ACROSS = 4
 CUTS = 2
-VMEM = 56 << 20
+VMEM = 32 << 20
 
 
 def near_docs(doc_ref, tok):
@@ -68,8 +68,8 @@
     return part[0:1]
 
 
-def whole_kernel(groups, chunk, depth, scales, doc_ref, w_ref, filt_ref, x_hbm, cot_hbm, out_hbm, gx_hbm, s_out, l_out,
-                 xs, cs, qs, ks, vs, pwin, gwin, mg, ys, outs, tail, mine, border, heads, ahead,
+def whole_kernel(groups, chunk, depth, scales, doc_hbm, w_hbm, filt_hbm, x_hbm, cot_hbm, out_hbm, gx_hbm, s_out, l_out,
+                 doc_ref, w_ref, filt_ref, table_sem, xs, cs, qs, ks, vs, pwin, gwin, mg, ys, outs, tail, mine, border, heads, ahead,
                  back_shift, fore_shift, back_edge, fore_edge, keeps, keeps32, wide_filt, ssum, lsum,
                  s1, l1, s2, l2, s3, l3, bs, bl,
                  tail_sem, in_sem, out_sem, y_sem, edge_sem, blk_send, blk_recv, row_send, row_recv, x_send, x_recv, z_sem, send, recv):
@@ -157,6 +157,9 @@
 
     first = pltpu.make_async_copy(x_hbm.at[tok - 16 :, :], tail, tail_sem)
     first.start()
+    pairs = ((doc_hbm, doc_ref), (filt_hbm, filt_ref), (w_hbm, w_ref))
+    tables = [pltpu.make_async_copy(src, dst, table_sem.at[n]) for n, (src, dst) in enumerate(pairs)]
+    begin(tables)
     for i in range(count):
         begin(loads(i))
     peers = [right, left] + across + along + final
@@ -169,6 +172,8 @@
     edge_copy = sent(mine, border, edge_sem.at[0], edge_sem.at[1], right)
     edge_copy.start()
 
+    for copy in tables:
+        copy.wait()
     docs = near_docs(doc_ref, tok)
     own = docs[:, tok : 2 * tok]
     col = doc_column(own)
@@ -177,11 +182,12 @@
         shifts[tok:, :] = shift_matrix(col, own, 2 * sign)
     row = lax.broadcasted_iota(jnp.int32, (8, LANES), 0)
     spread_doc = lambda d: jnp.broadcast_to(docs[:, d : d + 1], (8, LANES))
-    top, end = col[:8, :], col[tok - 8 :, :]
-    old, new = [spread_doc(tok - 1), spread_doc(tok - 2)], [spread_doc(2 * tok), spread_doc(2 * tok + 1)]
-    back_edge[0] = jnp.where((row == 0) & (top == old[0]), 1.0, 0.0)
-    back_edge[1] = jnp.where((row == 0) & (top == old[1]), 1.0, 0.0)
-    back_edge[2] = jnp.where((row == 1) & (top == old[0]), 1.0, 0.0)
+    end = col[tok - 8 :, :]
+    new = [spread_doc(2 * tok), spread_doc(2 * tok + 1)]
+    past = jnp.concatenate([docs, jnp.full((1, tok), -3.0, F32)], axis=1)
+    for n in range(2):
+        earlier = pltpu.roll(jnp.broadcast_to(past, (8, 4 * tok)), n + 1, 1)[0:1, tok : 2 * tok]
+        back_edge[n] = jnp.where(col[:16, :] == doc_column(earlier)[:16, :], 1.0, 0.0)
     fore_edge[0] = jnp.where((row == 7) & (end == new[0]), 1.0, 0.0)
     fore_edge[1] = jnp.where((row == 6) & (end == new[0]), 1.0, 0.0)
     fore_edge[2] = jnp.where((row == 7) & (end == new[1]), 1.0, 0.0)
@@ -204,18 +210,12 @@
     wide_filt[:, tok : 2 * tok] = jnp.where(lane == 0, filt, 0.0)
     wide_filt[:, 2 * tok : 3 * tok] = filt
     wide_filt[:, 3 * tok :] = jnp.zeros(filt.shape, F32)
-    edge_copy.wait()
-
     def mixed(i, j, part):
         here = pl.ds(pl.multiple_of(part * width + i * chunk + j * wide, LANES), wide)
-        edges = [jnp.concatenate([back_edge[n]] * 2, axis=1) for n in range(3)]
         value = xs[:, here]
         moved = jnp.dot(back_shift[...], value, preferred_element_type=F32)
-        side = border[:, here].astype(F32)
         w = w_ref[:, here]
-        mix = w[0:1] * value.astype(F32) + w[1:2] * moved[:tok] + w[2:3] * moved[tok:]
-        fix = w[1:2] * (edges[0] * side[1:2]) + w[2:3] * (edges[1] * side[0:1] + edges[2] * side[1:2])
-        return jnp.concatenate([mix[:8] + fix, mix[8:]], axis=0).astype(BF)
+        return (w[0:1] * value.astype(F32) + w[1:2] * moved[:tok] + w[2:3] * moved[tok:]).astype(BF)
 
     def mix_step(i, carry):
         for copy in loads(i):
@@ -226,10 +226,37 @@
             qs[:, here], ks[:, here], vs[:, here] = q, k, v
             gwin[0:tok, here] = (cs[:, here].astype(F32) * q.astype(F32)).astype(BF)
             pwin[tok : 2 * tok, here] = (k.astype(F32) * v.astype(F32)).astype(BF)
+        return carry
+
+    def top_rows(i, part):
+        here = at(i, offset=part * width)
+        place_row = lax.broadcasted_iota(jnp.int32, (16, chunk), 0)
+        keep = [jnp.concatenate([back_edge[n]] * (chunk // LANES), axis=1) for n in range(2)]
+        value = xs[0:16, here].astype(F32)
+        side = border[:, here].astype(F32)
+        one = jnp.where(place_row == 0, side[1:2], pltpu.roll(value, 1, 0))
+        two = jnp.where(place_row == 0, side[0:1], jnp.where(place_row == 1, side[1:2], pltpu.roll(value, 2, 0)))
+        w = w_ref[:, here]
+        return (w[0:1] * value + w[1:2] * (keep[0] * one) + w[2:3] * (keep[1] * two)).astype(BF)
+
+    def fix_step(i, carry):
+        here = at(i)
+        q, k, v = top_rows(i, 0), top_rows(i, 1), top_rows(i, 2)
+        qs[0:16, here], ks[0:16, here], vs[0:16, here] = q, k, v
+        gwin[0:16, here] = (cs[0:16, here].astype(F32) * q.astype(F32)).astype(BF)
+        pwin[tok : tok + 16, here] = (k.astype(F32) * v.astype(F32)).astype(BF)
+        return carry
+
+    middle, ready = count // 2, count
+    lax.fori_loop(0, middle, mix_step, 0)
+    edge_copy.wait()
+    for i in range(middle):
+        fix_step(i, 0)
         begin(block_sends(i))
-        return carry
-
-    lax.fori_loop(0, count, mix_step, 0)
+    lax.fori_loop(middle, count, mix_step, 0)
+    for i in range(middle, count):
+        fix_step(i, 0)
+        begin(block_sends(i))
 
     lane_group = lax.broadcasted_iota(jnp.int32, (rows, LANES), 1) // (LANES // groups)
 
@@ -243,6 +270,10 @@
     per_x = per_z // ACROSS
 
     def long_step(i, carry):
+        @pl.when(i + ready < count)
+        def _():
+            begin(block_sends(i + ready))
+
         arrive(block_sends(i))
         for j in range(blocks):
             part = [pl.ds(pl.multiple_of(p * width + i * chunk + j * LANES, LANES), LANES) for p in range(3)]
@@ -406,6 +437,7 @@
     dma = pltpu.SemaphoreType.DMA
     half = lambda *s: pltpu.VMEM(s, BF)
     word = lambda *s: pltpu.VMEM(s, F32)
+    doc_ids, short_filter, long_filter, x, cot = [pltpu.with_memory_space_constraint(a, pltpu.HBM) for a in (doc_ids, short_filter, long_filter, x, cot)]
     out, gx, gs, gl = pl.pallas_call(
         functools.partial(whole_kernel, LANES // (width // groups), chunk, depth, scales),
         out_shape=[
@@ -414,13 +446,14 @@
             jax.ShapeDtypeStruct((3, pair // CORES), F32),
             jax.ShapeDtypeStruct((some // CORES, taps), F32),
         ],
-        in_specs=[space] * 3 + [far] * 2,
+        in_specs=[pl.BlockSpec(memory_space=pltpu.HBM)] * 5,
         out_specs=[far, far, space, space],
         scratch_shapes=[
+            pltpu.VMEM(doc_ids.shape, jnp.int32), word(3, full), half(groups, taps), dma((3,)),
             half(tok, full), half(tok, width), half(tok, width), half(tok, width), half(tok, width),
             half(3 * tok, width), half(3 * tok, width), half(tok, full), half(tok, full), half(tok, width),
             half(16, full), half(2, full), half(2, full), half(2, full), half(2, full),
-            half(2 * tok, tok), half(2 * tok, tok), word(3, 8, LANES), word(3, 8, LANES),
+            half(2 * tok, tok), half(2 * tok, tok), word(2, 16, LANES), word(3, 8, LANES),
             half(2 * tok, 2 * tok), word(2 * tok, 2 * tok), word(groups, 4 * tok),
             word(ACROSS, depth, 3, pair), word(ACROSS, depth, some, taps),
             word(ACROSS - 1, depth, 3, pair), word(ACROSS - 1, depth, some, taps),

time: 61.9 us -> 58.9 us (0.952)
  Pallas kernels: 61.1 us -> 58.2 us
    pallas_call x1, Pallas kernels: 3.75 us -> 2.18 us  [copied(): pl.pallas_call(copy_kernel, grid=(cuts,), out_shape=[jax.ShapeDtypeStruct...]
    pallas_call x1, Pallas kernels: 57.4 us -> 56 us  [local(): pl.pallas_call(functools.partial(whole_kernel, LANES // (width // groups)...]
where the time goes in v5:
time: 58.9 us; the launch traced here: 58.8 us
  Pallas kernels  58.2 us (99%)
  between operations  0.64 us (1%)
    pallas_call x1, Pallas kernels, local(): pl.pallas_call(functools.partial(whole_kernel, LANES // (width // groups)...  56 us
    pallas_call x1, Pallas kernels, copied(): pl.pallas_call(copy_kernel, grid=(cuts,), out_shape=[jax.ShapeDtypeStruct...  2.18 us

profile of v5, /device:TPU:1, one launch (start us, length us, event | category | flops | bytes accessed | tf_op | source)
XLA Modules:
  0.0 58.8 jit_solution(13742506719711688584)
XLA Ops:
  0.6 56.0 %whole.1 = (bf16[128,4096]{1,0:T(8,128)(2,1)S(1)}, bf16[128,12288]{1,0:T(8,128)(2,1)S(1)}, f32[3,192]{1,0:T(4,128)S(1)}, f32[4,128]{1,0:T(4,128)S(1)}) custom-call(s32[1,8192]{1,0:T(1,128)} %doc_hbm.1, f32[3,12288]{1,0:T(4,128)} %w_hbm.1, bf16[256,128]{1,0:T(8,128)(2,1)} %filt_hbm.1, bf16[128,12288]{1,0:T(8,128)(2,1)} %bitcast.4, bf16[128,4096]{1,0:T(8,128)(2,1)} %bitcast.5), custom_call_target="tpu_custom_call" | custom-call | tf_op jit(solution)/shard_map/whole/pallas_call | solution.py:441
  56.6 2.2 %place.1 = (bf16[128,4096]{1,0:T(8,128)(2,1)}, bf16[128,12288]{1,0:T(8,128)(2,1)}, f32[3,192]{1,0:T(4,128)}, f32[4,128]{1,0:T(4,128)}) custom-call(bf16[128,4096]{1,0:T(8,128)(2,1)S(1)} %get-tuple-element.12.refs_0_, bf16[128,12288]{1,0:T(8,128)(2,1)S(1)} %get-tuple-element.13.refs_1_, f32[3,192]{1,0:T(4,128)S(1)} %get-tuple-element.14.refs_2_, ...), custom_call_target="tpu_custom_call" | custom-call | tf_op jit(solution)/shard_map/place/pallas_call | solution.py:410
